TPU v7x, 128 devices: a whole 4x4x4 slice. The times are simulated.
128 devices in a mesh: gx: 8 (over x, core), gy: 16 (over y, z).
Axes of the slice: x: 4, y: 4, z: 4, core: 2. Of those that a mesh axis runs over, the one named last changes fastest.
Arguments:
- flux: float32 [8, 512, 4096], P(None, 'gx', 'gy'), may hold values from -6 to 6
- diffusivity: float32 [256, 2048], P('gx', 'gy'), may hold values from 0.08 to 0.24
- remap_bank: bfloat16 [16, 3, 256, 128], replicated, may hold values from -0.21875 to 0.21875
- rec_owner: int32 [16384], P(('gx', 'gy')), may hold values from 0 to 127, as said below
- rec_source: int32 [16384], P(('gx', 'gy')), may hold values from 0 to 63
- rec_target: int32 [16384], P(('gx', 'gy')), may hold values from 0 to 31
- rec_weight: int32 [16384], P(('gx', 'gy')), may hold values from 0 to 15
Outputs:
- ocean_state: float32 [8, 256, 2048], P(None, 'gx', 'gy')
Inputs may be any that keep to these rules, and one draw needn't show every extreme that they name: `rec_owner`: among the records of one atmosphere block each owner appears at most 2 times; in every draw some owner appears exactly 2 times in every block's records.
All inputs are finite; a program needn't handle non-finite values.
Results may differ from a plain program's by a relative error of at most 0.0029.
Values may be sent and summed in bfloat16 or wider, within the bound.
No kernel may reach another device: no remote copies, remote signals or barrier semaphores. Data moves between devices by JAX's collectives and lax.ppermute only.
A program may use at most 64 MiB of HBM per device.

v0:
```python
import math

import jax
import jax.numpy as jnp
from jax import lax
from jax.sharding import PartitionSpec as P

TILE_X = 16
TILE_Y = 16
OTILE_X = 8
OTILE_Y = 16
SWEEPS = 4


def extended(cells, sides, width, closed):
    for axis, dim in sides:
        count = lax.axis_size(axis)
        ends = count if closed else count - 1
        head = lax.slice_in_dim(cells, 0, width, axis=dim)
        tail = lax.slice_in_dim(cells, cells.shape[dim] - width, cells.shape[dim], axis=dim)
        cells = jnp.concatenate(
            [
                lax.ppermute(tail, axis, [(i, (i + 1) % count) for i in range(ends)]),
                cells,
                lax.ppermute(head, axis, [((i + 1) % count, i) for i in range(ends)]),
            ],
            axis=dim,
        )
    return cells


def block_products(source_part, weight_ids, remap_bank):
    bank_part = remap_bank[jnp.maximum(weight_ids, 0)]
    return jnp.einsum("gkfc,gkco->gfo", source_part, bank_part, preferred_element_type=jnp.float32)


def remap_slots(arrived, target_ids, weight_ids, remap_bank, tile_ids):
    slot_count = arrived.shape[0]
    group_size = math.gcd(slot_count, 32)
    block_count = slot_count // group_size
    fields = arrived.shape[2]
    out_cells = remap_bank.shape[3]

    def accumulate(total, pieces):
        source_part, dest_ids, bank_ids = pieces
        contribution = block_products(source_part, bank_ids, remap_bank)
        onehot = (dest_ids[:, None] == tile_ids[None, :]).astype(jnp.float32)
        return (
            total
            + jnp.einsum("gt,gfo->tfo", onehot, contribution, precision=lax.Precision.HIGHEST),
            None,
        )

    start_total = jnp.zeros((tile_ids.shape[0], fields, out_cells), jnp.float32)
    total, unused = lax.scan(
        accumulate,
        start_total,
        (
            arrived.reshape((block_count, group_size) + arrived.shape[1:]),
            target_ids.reshape(block_count, group_size),
            weight_ids.reshape(block_count, group_size),
        ),
    )
    return total


def ocean_grid(forcing, grid_rows, grid_cols):
    fields = forcing.shape[1]
    tiles_x = grid_rows // OTILE_X
    tiles_y = grid_cols // OTILE_Y
    shaped = forcing.reshape(tiles_x, tiles_y, fields, OTILE_X, OTILE_Y)
    return shaped.transpose(2, 0, 3, 1, 4).reshape(fields, grid_rows, grid_cols)


def local(flux, diffusivity, remap_bank, rec_owner, rec_source, rec_target, rec_weight):
    fields, grid_rows, grid_cols = flux.shape
    padded = extended(flux, (("gx", 1), ("gy", 2)), 1, True)
    slope_x = (padded[:, 2:, 1:-1] - padded[:, :-2, 1:-1]) * 0.5
    slope_y = (padded[:, 1:-1, 2:] - padded[:, 1:-1, :-2]) * 0.5
    coeffs = jnp.stack([flux, slope_x, slope_y]).astype(jnp.bfloat16)
    tile_cells = TILE_X * TILE_Y
    source_tiles = coeffs.reshape(
        3, fields, grid_rows // TILE_X, TILE_X, grid_cols // TILE_Y, TILE_Y
    )
    source_tiles = source_tiles.transpose(2, 4, 0, 1, 3, 5).reshape(-1, 3, fields, tile_cells)
    owners = lax.axis_size(("gx", "gy"))
    records = rec_owner.shape[0]
    capacity = max(2, 2 * records // owners)
    slot_count = owners * capacity
    owner_ids = jnp.arange(owners, dtype=jnp.int32)
    member = (rec_owner[:, None] == owner_ids[None, :]).astype(jnp.int32)
    before = jnp.cumsum(member, axis=0) - member
    slot_rank = jnp.sum(before * member, axis=1)
    slot_of = rec_owner * capacity + slot_rank
    ocean_rows, ocean_cols = diffusivity.shape
    tile_total = ocean_rows // OTILE_X * (ocean_cols // OTILE_Y)
    tile_ids = jnp.arange(tile_total, dtype=jnp.int32)
    picked = source_tiles[rec_source]
    outgoing = jnp.zeros((slot_count,) + picked.shape[1:], jnp.bfloat16).at[slot_of].set(picked)
    labels = (
        jnp.full((slot_count, 2), -1, jnp.int32)
        .at[slot_of]
        .set(jnp.stack([rec_target, rec_weight], axis=1))
    )
    arrived, arrived_labels = (
        lax.all_to_all(outgoing, ("gx", "gy"), split_axis=0, concat_axis=0, tiled=True),
        lax.all_to_all(labels, ("gx", "gy"), split_axis=0, concat_axis=0, tiled=True),
    )
    forcing = remap_slots(arrived, arrived_labels[:, 0], arrived_labels[:, 1], remap_bank, tile_ids)
    ocean = ocean_grid(forcing, ocean_rows, ocean_cols)
    for sweep in range(SWEEPS):
        bordered = extended(ocean, (("gx", 1), ("gy", 2)), 1, False)
        beside_all = (
            bordered[:, 2:, 1:-1]
            + bordered[:, :-2, 1:-1]
            + bordered[:, 1:-1, 2:]
            + bordered[:, 1:-1, :-2]
        )
        ocean = ocean + diffusivity * (beside_all - 4.0 * ocean)
    return ocean


def solution(mesh):
    in_specs = (
        P(None, "gx", "gy"),
        P("gx", "gy"),
        P(),
        P(("gx", "gy")),
        P(("gx", "gy")),
        P(("gx", "gy")),
        P(("gx", "gy")),
    )
    out_specs = P(None, "gx", "gy")
    return jax.shard_map(local, mesh=mesh, in_specs=in_specs, out_specs=out_specs, check_vma=False)
```

profile of v0, /device:TPU:10, one launch (start us, length us, event | category | flops | bytes accessed | tf_op | source)
XLA Modules:
  0.0 267.7 jit_solution(5739370391608427125)
XLA Ops:
  0.0 0.9 fusion.46
  4.7 0.9 scatter_custom_fusion
  5.6 1.5 copy.18
  7.1 12.0 %all-to-all-start = ((s32[128,2,2]{1,2,0:T(2,128)}), s32[128,2,2]{1,2,0:T(2,128)S(1)}, u32[]{:S(2)}, u32[]{:S(2)}) async-start(s32[128,2,2]{1,2,0:T(2,128)} %copy.18), calls=%async_computation | async-start | bytes 262144 | tf_op jit(solution)/shard_map/all_to_all | solution.py:107
  19.8 1.1 pad_maximum_fusion
  21.1 3.4 %collective-permute-start.2 = (f32[8,66,1]{2,1,0:T(8,128)S(1)}, f32[8,66,1]{2,1,0:T(8,128)S(1)}, u32[]{:S(2)}, u32[]{:S(2)}) collective-permute-start(f32[8,66,1]{2,1,0:T(8,128)S(1)} %get-tuple-element.82), channel_id=1, source_target_pairs={{1,0},{2,1},{3,2},{4,3},{5,4},{6,5},{7,6},{8,7},{9,8},{10,9},{11,1... | collective-permute-start | bytes 6344 | tf_op jit(solution)/shard_map/ppermute | solution.py:25
  24.5 6.5 %collective-permute-done.2 = f32[8,66,1]{2,1,0:T(8,128)S(1)} collective-permute-done((f32[8,66,1]{2,1,0:T(8,128)S(1)}, f32[8,66,1]{2,1,0:T(8,128)S(1)}, u32[]{:S(2)}, u32[]{:S(2)}) %collective-permute-start.2) | collective-permute-done | bytes 2144 | tf_op jit(solution)/shard_map/ppermute | solution.py:25
  31.0 4.3 %collective-permute-done.3 = f32[8,66,1]{2,1,0:T(8,128)S(1)} collective-permute-done((f32[8,66,1]{2,1,0:T(8,128)S(1)}, f32[8,66,1]{2,1,0:T(8,128)S(1)}, u32[]{:S(2)}, u32[]{:S(2)}) %collective-permute-start.3) | collective-permute-done | bytes 2144 | tf_op jit(solution)/shard_map/ppermute | solution.py:23
  35.9 1.4 stack.24
  37.3 1.8 copy.20
  39.2 1.4 stack.25
  40.6 1.9 copy.21
  42.5 1.4 stack.26
  44.5 1.0 copy-done.1
  46.1 4.0 %maximum_bitcast_fusion = bf16[4,16,3,8,16,16]{5,4,3,2,1,0:T(8,128)(2,1)} fusion(bf16[1,8,4,16,16,16]{5,3,1,0,4,2:T(8,128)(2,1)S(1)} %copy.22, bf16[1,8,4,16,16,16]{5,3,1,0,4,2:T(8,128)(2,1)S(1)} %copy-done.2, bf16[1,8,4,16,16,16]{5,3,1,0,4,2:T(8,128)(2,1)S(1)} %copy-done.1), kind=kLoop, calls=%fused_computation.20 | loop fusion | flops 786432 | bytes 1572864 | tf_op jit(solution)/shard_map/transpose | solution.py:85
  50.1 7.8 %reshape.41 = bf16[64,3,8,256]{3,2,1,0:T(8,128)(2,1)S(1)} reshape(bf16[4,16,3,8,16,16]{5,4,3,2,1,0:T(8,128)(2,1)} %maximum_bitcast_fusion) | data formatting | bytes 1572864 | tf_op jit(solution)/shard_map/reshape | solution.py:85
  58.6 1.8 broadcast_in_dim.16
  60.4 15.6 %scatter_fusion = bf16[256,3,8,256]{3,2,1,0:T(8,128)(2,1)} fusion(bf16[256,3,8,256]{3,2,1,0:T(8,128)(2,1)} %broadcast_in_dim.16, s32[128]{0:T(128)S(1)} %compare_select_fusion.1, bf16[128,3,8,256]{3,2,1,0:T(8,128)(2,1)S(1)} %gather_fusion.1), kind=kCustom, calls=%fused_computation.3 | custom fusion | bytes 4719104 | tf_op jit(solution)/shard_map/scatter | solution.py:99
  76.0 8.9 %all-to-all-start.1 = ((bf16[256,3,8,256]{3,2,1,0:T(8,128)(2,1)}), bf16[256,3,8,256]{3,2,1,0:T(8,128)(2,1)}, u32[]{:S(2)}, u32[]{:S(2)}) async-start(bf16[256,3,8,256]{3,2,1,0:T(8,128)(2,1)} %scatter_fusion), calls=%async_computation.1 | async-start | bytes 6291456 | tf_op jit(solution)/shard_map/all_to_all | solution.py:106
  85.3 39.0 %all-to-all-done.1 = bf16[256,3,8,256]{3,2,1,0:T(8,128)(2,1)} async-done(((bf16[256,3,8,256]{3,2,1,0:T(8,128)(2,1)}), bf16[256,3,8,256]{3,2,1,0:T(8,128)(2,1)}, u32[]{:S(2)}, u32[]{:S(2)}) %all-to-all-start.1) | async-done | bytes 3145760 | tf_op jit(solution)/shard_map/all_to_all | solution.py:106
  124.3 65.0 %while.11 = (s32[]{:T(128)}, f32[32,8,128]{2,0,1:T(8,128)S(1)}, s32[8,32]{1,0:T(8,128)S(1)}, bf16[8,32,3,8,256]{4,3,2,1,0:T(8,128)(2,1)}, s32[8,32]{1,0:T(8,128)...) while((s32[]{:T(128)}, f32[32,8,128]{2,0,1:T(8,128)S(1)}, ...), condition=%wide.region_5.6_spmd.clone, body=%wide.region_4.5_spmd.clone.sunk | while | flops 62982176 | bytes 19797472 | solution.py:55
  124.3 4.0 %gather_fusion = bf16[32,3,256,128]{3,2,1,0:T(8,128)(2,1)} fusion(bf16[16,3,256,128]{3,2,1,0:T(8,128)(2,1)S(1)} %get-tuple-element.167, s32[1024]{0:T(1024)S(1)} %pad_clamp_fusion.3), kind=kCustom, calls=%fused_computation.clone.clone.1 | custom fusion | bytes 12583040 | tf_op jit(solution)/shard_map/while/body/eval_jaxpr/gather | solution.py:33
  128.3 3.9 %convolution_bitcast_fusion.2 = f32[32,8,128]{2,1,0:T(8,128)S(1)} fusion(bf16[32,3,256,128]{3,2,1,0:T(8,128)(2,1)} %gather_fusion, bf16[8,32,3,8,256]{4,3,2,1,0:T(8,128)(2,1)} %get-tuple-element.165, s32[]{:T(128)} %get-tuple-element.154), kind=kOutput, calls=%fused_computation.5.clone.1 | convolution fusion | flops 50331648 | bytes 6816256 | tf_op jit(solution)/shard_map/while/body/eval_jaxpr/gkfc,gkco->gfo/dot_general | solution.py:34
  132.5 4.0 %gather_fusion = bf16[32,3,256,128]{3,2,1,0:T(8,128)(2,1)} fusion(bf16[16,3,256,128]{3,2,1,0:T(8,128)(2,1)S(1)} %get-tuple-element.167, s32[1024]{0:T(1024)S(1)} %pad_clamp_fusion.3), kind=kCustom, calls=%fused_computation.clone.clone.1 | custom fusion | bytes 12583040 | tf_op jit(solution)/shard_map/while/body/eval_jaxpr/gather | solution.py:33
  136.5 3.9 %convolution_bitcast_fusion.2 = f32[32,8,128]{2,1,0:T(8,128)S(1)} fusion(bf16[32,3,256,128]{3,2,1,0:T(8,128)(2,1)} %gather_fusion, bf16[8,32,3,8,256]{4,3,2,1,0:T(8,128)(2,1)} %get-tuple-element.165, s32[]{:T(128)} %get-tuple-element.154), kind=kOutput, calls=%fused_computation.5.clone.1 | convolution fusion | flops 50331648 | bytes 6816256 | tf_op jit(solution)/shard_map/while/body/eval_jaxpr/gkfc,gkco->gfo/dot_general | solution.py:34
  140.6 4.0 %gather_fusion = bf16[32,3,256,128]{3,2,1,0:T(8,128)(2,1)} fusion(bf16[16,3,256,128]{3,2,1,0:T(8,128)(2,1)S(1)} %get-tuple-element.167, s32[1024]{0:T(1024)S(1)} %pad_clamp_fusion.3), kind=kCustom, calls=%fused_computation.clone.clone.1 | custom fusion | bytes 12583040 | tf_op jit(solution)/shard_map/while/body/eval_jaxpr/gather | solution.py:33
  144.6 3.9 %convolution_bitcast_fusion.2 = f32[32,8,128]{2,1,0:T(8,128)S(1)} fusion(bf16[32,3,256,128]{3,2,1,0:T(8,128)(2,1)} %gather_fusion, bf16[8,32,3,8,256]{4,3,2,1,0:T(8,128)(2,1)} %get-tuple-element.165, s32[]{:T(128)} %get-tuple-element.154), kind=kOutput, calls=%fused_computation.5.clone.1 | convolution fusion | flops 50331648 | bytes 6816256 | tf_op jit(solution)/shard_map/while/body/eval_jaxpr/gkfc,gkco->gfo/dot_general | solution.py:34
  148.7 4.0 %gather_fusion = bf16[32,3,256,128]{3,2,1,0:T(8,128)(2,1)} fusion(bf16[16,3,256,128]{3,2,1,0:T(8,128)(2,1)S(1)} %get-tuple-element.167, s32[1024]{0:T(1024)S(1)} %pad_clamp_fusion.3), kind=kCustom, calls=%fused_computation.clone.clone.1 | custom fusion | bytes 12583040 | tf_op jit(solution)/shard_map/while/body/eval_jaxpr/gather | solution.py:33
  152.7 3.9 %convolution_bitcast_fusion.2 = f32[32,8,128]{2,1,0:T(8,128)S(1)} fusion(bf16[32,3,256,128]{3,2,1,0:T(8,128)(2,1)} %gather_fusion, bf16[8,32,3,8,256]{4,3,2,1,0:T(8,128)(2,1)} %get-tuple-element.165, s32[]{:T(128)} %get-tuple-element.154), kind=kOutput, calls=%fused_computation.5.clone.1 | convolution fusion | flops 50331648 | bytes 6816256 | tf_op jit(solution)/shard_map/while/body/eval_jaxpr/gkfc,gkco->gfo/dot_general | solution.py:34
  156.8 4.0 %gather_fusion = bf16[32,3,256,128]{3,2,1,0:T(8,128)(2,1)} fusion(bf16[16,3,256,128]{3,2,1,0:T(8,128)(2,1)S(1)} %get-tuple-element.167, s32[1024]{0:T(1024)S(1)} %pad_clamp_fusion.3), kind=kCustom, calls=%fused_computation.clone.clone.1 | custom fusion | bytes 12583040 | tf_op jit(solution)/shard_map/while/body/eval_jaxpr/gather | solution.py:33
  160.8 3.9 %convolution_bitcast_fusion.2 = f32[32,8,128]{2,1,0:T(8,128)S(1)} fusion(bf16[32,3,256,128]{3,2,1,0:T(8,128)(2,1)} %gather_fusion, bf16[8,32,3,8,256]{4,3,2,1,0:T(8,128)(2,1)} %get-tuple-element.165, s32[]{:T(128)} %get-tuple-element.154), kind=kOutput, calls=%fused_computation.5.clone.1 | convolution fusion | flops 50331648 | bytes 6816256 | tf_op jit(solution)/shard_map/while/body/eval_jaxpr/gkfc,gkco->gfo/dot_general | solution.py:34
  165.0 4.0 %gather_fusion = bf16[32,3,256,128]{3,2,1,0:T(8,128)(2,1)} fusion(bf16[16,3,256,128]{3,2,1,0:T(8,128)(2,1)S(1)} %get-tuple-element.167, s32[1024]{0:T(1024)S(1)} %pad_clamp_fusion.3), kind=kCustom, calls=%fused_computation.clone.clone.1 | custom fusion | bytes 12583040 | tf_op jit(solution)/shard_map/while/body/eval_jaxpr/gather | solution.py:33
  169.0 3.9 %convolution_bitcast_fusion.2 = f32[32,8,128]{2,1,0:T(8,128)S(1)} fusion(bf16[32,3,256,128]{3,2,1,0:T(8,128)(2,1)} %gather_fusion, bf16[8,32,3,8,256]{4,3,2,1,0:T(8,128)(2,1)} %get-tuple-element.165, s32[]{:T(128)} %get-tuple-element.154), kind=kOutput, calls=%fused_computation.5.clone.1 | convolution fusion | flops 50331648 | bytes 6816256 | tf_op jit(solution)/shard_map/while/body/eval_jaxpr/gkfc,gkco->gfo/dot_general | solution.py:34
  173.1 4.0 %gather_fusion = bf16[32,3,256,128]{3,2,1,0:T(8,128)(2,1)} fusion(bf16[16,3,256,128]{3,2,1,0:T(8,128)(2,1)S(1)} %get-tuple-element.167, s32[1024]{0:T(1024)S(1)} %pad_clamp_fusion.3), kind=kCustom, calls=%fused_computation.clone.clone.1 | custom fusion | bytes 12583040 | tf_op jit(solution)/shard_map/while/body/eval_jaxpr/gather | solution.py:33
  177.1 3.9 %convolution_bitcast_fusion.2 = f32[32,8,128]{2,1,0:T(8,128)S(1)} fusion(bf16[32,3,256,128]{3,2,1,0:T(8,128)(2,1)} %gather_fusion, bf16[8,32,3,8,256]{4,3,2,1,0:T(8,128)(2,1)} %get-tuple-element.165, s32[]{:T(128)} %get-tuple-element.154), kind=kOutput, calls=%fused_computation.5.clone.1 | convolution fusion | flops 50331648 | bytes 6816256 | tf_op jit(solution)/shard_map/while/body/eval_jaxpr/gkfc,gkco->gfo/dot_general | solution.py:34
  181.2 4.0 %gather_fusion = bf16[32,3,256,128]{3,2,1,0:T(8,128)(2,1)} fusion(bf16[16,3,256,128]{3,2,1,0:T(8,128)(2,1)S(1)} %get-tuple-element.167, s32[1024]{0:T(1024)S(1)} %pad_clamp_fusion.3), kind=kCustom, calls=%fused_computation.clone.clone.1 | custom fusion | bytes 12583040 | tf_op jit(solution)/shard_map/while/body/eval_jaxpr/gather | solution.py:33
  185.2 3.9 %convolution_bitcast_fusion.2 = f32[32,8,128]{2,1,0:T(8,128)S(1)} fusion(bf16[32,3,256,128]{3,2,1,0:T(8,128)(2,1)} %gather_fusion, bf16[8,32,3,8,256]{4,3,2,1,0:T(8,128)(2,1)} %get-tuple-element.165, s32[]{:T(128)} %get-tuple-element.154), kind=kOutput, calls=%fused_computation.5.clone.1 | convolution fusion | flops 50331648 | bytes 6816256 | tf_op jit(solution)/shard_map/while/body/eval_jaxpr/gkfc,gkco->gfo/dot_general | solution.py:34
  190.1 1.9 collective-permute-start.4
  192.1 2.4 collective-permute-start.5
  194.5 2.7 %collective-permute-done.5 = f32[8,1,128]{2,1,0:T(1,128)S(1)} collective-permute-done((f32[8,1,128]{2,1,0:T(1,128)S(1)}, f32[8,1,128]{2,1,0:T(1,128)S(1)}, u32[]{:S(2)}, u32[]{:S(2)}) %collective-permute-start.5) | collective-permute-done | bytes 4128 | tf_op jit(solution)/shard_map/ppermute | solution.py:23
  197.4 4.5 %collective-permute-start.6 = (f32[8,34,1]{2,1,0:T(8,128)S(1)}, f32[8,34,1]{2,1,0:T(8,128)S(1)}, u32[]{:S(2)}, u32[]{:S(2)}) collective-permute-start(f32[8,34,1]{2,1,0:T(8,128)S(1)} %get-tuple-element.95), channel_id=1, source_target_pairs={{1,0},{2,1},{3,2},{4,3},{5,4},{6,5},{7,6},{8,7},{9,8},{10,9},{11,1... | collective-permute-start | bytes 3272 | tf_op jit(solution)/shard_map/ppermute | solution.py:25
  201.9 1.9 collective-permute-start.7
  204.7 6.5 %collective-permute-done.7 = f32[8,34,1]{2,1,0:T(8,128)S(1)} collective-permute-done((f32[8,34,1]{2,1,0:T(8,128)S(1)}, f32[8,34,1]{2,1,0:T(8,128)S(1)}, u32[]{:S(2)}, u32[]{:S(2)}) %collective-permute-start.7) | collective-permute-done | bytes 1120 | tf_op jit(solution)/shard_map/ppermute | solution.py:23
  211.4 1.9 collective-permute-start.8
  213.3 2.4 collective-permute-start.9
  215.8 2.5 collective-permute-done.9
  218.4 1.9 collective-permute-start.10
  220.3 3.9 %collective-permute-start.11 = (f32[8,34,1]{2,1,0:T(8,128)S(1)}, f32[8,34,1]{2,1,0:T(8,128)S(1)}, u32[]{:S(2)}, u32[]{:S(2)}) collective-permute-start(f32[8,34,1]{2,1,0:T(8,128)S(1)} %get-tuple-element.94), channel_id=1, source_target_pairs={{0,1},{1,2},{2,3},{3,4},{4,5},{5,6},{6,7},{7,8},{8,9},{9,10},{10,1... | collective-permute-start | bytes 3272 | tf_op jit(solution)/shard_map/ppermute | solution.py:23
  224.3 1.4 collective-permute-done.10
  225.6 4.0 %collective-permute-done.11 = f32[8,34,1]{2,1,0:T(8,128)S(1)} collective-permute-done((f32[8,34,1]{2,1,0:T(8,128)S(1)}, f32[8,34,1]{2,1,0:T(8,128)S(1)}, u32[]{:S(2)}, u32[]{:S(2)}) %collective-permute-start.11) | collective-permute-done | bytes 1120 | tf_op jit(solution)/shard_map/ppermute | solution.py:23
  229.9 2.1 collective-permute-start.12
  232.0 2.2 collective-permute-start.13
  234.2 2.7 %collective-permute-done.13 = f32[8,1,128]{2,1,0:T(1,128)S(1)} collective-permute-done((f32[8,1,128]{2,1,0:T(1,128)S(1)}, f32[8,1,128]{2,1,0:T(1,128)S(1)}, u32[]{:S(2)}, u32[]{:S(2)}) %collective-permute-start.13) | collective-permute-done | bytes 4128 | tf_op jit(solution)/shard_map/ppermute | solution.py:23
  237.1 1.9 collective-permute-start.14
  239.0 3.9 %collective-permute-start.15 = (f32[8,34,1]{2,1,0:T(8,128)S(1)}, f32[8,34,1]{2,1,0:T(8,128)S(1)}, u32[]{:S(2)}, u32[]{:S(2)}) collective-permute-start(f32[8,34,1]{2,1,0:T(8,128)S(1)} %get-tuple-element.92), channel_id=1, source_target_pairs={{0,1},{1,2},{2,3},{3,4},{4,5},{5,6},{6,7},{7,8},{8,9},{9,10},{10,1... | collective-permute-start | bytes 3272 | tf_op jit(solution)/shard_map/ppermute | solution.py:23
  242.9 1.4 collective-permute-done.14
  244.3 4.0 %collective-permute-done.15 = f32[8,34,1]{2,1,0:T(8,128)S(1)} collective-permute-done((f32[8,34,1]{2,1,0:T(8,128)S(1)}, f32[8,34,1]{2,1,0:T(8,128)S(1)}, u32[]{:S(2)}, u32[]{:S(2)}) %collective-permute-start.15) | collective-permute-done | bytes 1120 | tf_op jit(solution)/shard_map/ppermute | solution.py:23
  248.5 2.0 collective-permute-start.16
  250.5 2.3 collective-permute-start.17
  252.9 2.6 collective-permute-done.17
  255.6 1.9 collective-permute-start.18
  257.5 3.9 %collective-permute-start.19 = (f32[8,34,1]{2,1,0:T(8,128)S(1)}, f32[8,34,1]{2,1,0:T(8,128)S(1)}, u32[]{:S(2)}, u32[]{:S(2)}) collective-permute-start(f32[8,34,1]{2,1,0:T(8,128)S(1)} %get-tuple-element.90), channel_id=1, source_target_pairs={{0,1},{1,2},{2,3},{3,4},{4,5},{5,6},{6,7},{7,8},{8,9},{9,10},{10,1... | collective-permute-start | bytes 3272 | tf_op jit(solution)/shard_map/ppermute | solution.py:23
  261.4 1.4 collective-permute-done.18
  262.8 4.0 %collective-permute-done.19 = f32[8,34,1]{2,1,0:T(8,128)S(1)} collective-permute-done((f32[8,34,1]{2,1,0:T(8,128)S(1)}, f32[8,34,1]{2,1,0:T(8,128)S(1)}, u32[]{:S(2)}, u32[]{:S(2)}) %collective-permute-start.19) | collective-permute-done | bytes 1120 | tf_op jit(solution)/shard_map/ppermute | solution.py:23
  (81 shorter events, 12.7 us)
Async XLA Ops:
  0.0 35.3 %copy-start.3 = (f32[8,64,256]{2,1,0:T(8,128)S(1)}, f32[8,64,256]{2,1,0:T(8,128)}, u32[]{:S(2)}) copy-start(f32[8,64,256]{2,1,0:T(8,128)} %param.9) | copy-start | bytes 1572868
  0.9 18.9 %collective-permute-start = (f32[8,1,256]{2,1,0:T(1,128)S(1)}, f32[8,1,256]{2,1,0:T(1,128)S(1)}, u32[]{:S(2)}, u32[]{:S(2)}) collective-permute-start(f32[8,1,256]{2,1,0:T(1,128)S(1)} %get-tuple-element.88), channel_id=1, source_target_pairs={{16,0},{32,16},{48,32},{64,48},{80,64},{96,80},{112,96},{0,112},{1... | collective-permute-start | bytes 24584 | tf_op jit(solution)/shard_map/ppermute | solution.py:25
  1.0 18.8 %collective-permute-start.1 = (f32[8,1,256]{2,1,0:T(1,128)S(1)}, f32[8,1,256]{2,1,0:T(1,128)S(1)}, u32[]{:S(2)}, u32[]{:S(2)}) collective-permute-start(f32[8,1,256]{2,1,0:T(1,128)S(1)} %get-tuple-element.87), channel_id=1, source_target_pairs={{0,16},{16,32},{32,48},{48,64},{64,80},{80,96},{96,112},{112,0},{1... | collective-permute-start | bytes 24584 | tf_op jit(solution)/shard_map/ppermute | solution.py:23
  7.1 68.9 %all-to-all-start = ((s32[128,2,2]{1,2,0:T(2,128)}), s32[128,2,2]{1,2,0:T(2,128)S(1)}, u32[]{:S(2)}, u32[]{:S(2)}) async-start(s32[128,2,2]{1,2,0:T(2,128)} %copy.18), calls=%async_computation | async-start | bytes 262144 | tf_op jit(solution)/shard_map/all_to_all | solution.py:107
  21.1 10.0 %collective-permute-start.2 = (f32[8,66,1]{2,1,0:T(8,128)S(1)}, f32[8,66,1]{2,1,0:T(8,128)S(1)}, u32[]{:S(2)}, u32[]{:S(2)}) collective-permute-start(f32[8,66,1]{2,1,0:T(8,128)S(1)} %get-tuple-element.82), channel_id=1, source_target_pairs={{1,0},{2,1},{3,2},{4,3},{5,4},{6,5},{7,6},{8,7},{9,8},{10,9},{11,1... | collective-permute-start | bytes 6344 | tf_op jit(solution)/shard_map/ppermute | solution.py:25
  24.5 10.9 %collective-permute-start.3 = (f32[8,66,1]{2,1,0:T(8,128)S(1)}, f32[8,66,1]{2,1,0:T(8,128)S(1)}, u32[]{:S(2)}, u32[]{:S(2)}) collective-permute-start(f32[8,66,1]{2,1,0:T(8,128)S(1)} %get-tuple-element.83), channel_id=1, source_target_pairs={{0,1},{1,2},{2,3},{3,4},{4,5},{5,6},{6,7},{7,8},{8,9},{9,10},{10,1... | collective-permute-start | bytes 6344 | tf_op jit(solution)/shard_map/ppermute | solution.py:23
  43.9 1.6 copy-start.1
  43.9 2.2 copy-start.2
  76.0 48.3 %copy-start = (bf16[16,3,256,128]{3,2,1,0:T(8,128)(2,1)S(1)}, bf16[16,3,256,128]{3,2,1,0:T(8,128)(2,1)}, u32[]{:S(2)}) copy-start(bf16[16,3,256,128]{3,2,1,0:T(8,128)(2,1)} %param.11) | copy-start | bytes 9437188
  76.0 48.3 %all-to-all-start.1 = ((bf16[256,3,8,256]{3,2,1,0:T(8,128)(2,1)}), bf16[256,3,8,256]{3,2,1,0:T(8,128)(2,1)}, u32[]{:S(2)}, u32[]{:S(2)}) async-start(bf16[256,3,8,256]{3,2,1,0:T(8,128)(2,1)} %scatter_fusion), calls=%async_computation.1 | async-start | bytes 6291456 | tf_op jit(solution)/shard_map/all_to_all | solution.py:106
  189.3 21.9 %copy-start.4 = (f32[32,128]{1,0:T(8,128)S(1)}, f32[32,128]{1,0:T(8,128)}, u32[]{:S(2)}) copy-start(f32[32,128]{1,0:T(8,128)} %param.10) | copy-start | bytes 49156
  190.1 4.3 %collective-permute-start.4 = (f32[8,1,128]{2,1,0:T(1,128)S(1)}, f32[8,1,128]{2,1,0:T(1,128)S(1)}, u32[]{:S(2)}, u32[]{:S(2)}) collective-permute-start(f32[8,1,128]{2,1,0:T(1,128)S(1)} %get-tuple-element.104), channel_id=1, source_target_pairs={{16,0},{32,16},{48,32},{64,48},{80,64},{96,80},{112,96},{17,1},{33... | collective-permute-start | bytes 12296 | tf_op jit(solution)/shard_map/ppermute | solution.py:25
  192.1 5.1 %collective-permute-start.5 = (f32[8,1,128]{2,1,0:T(1,128)S(1)}, f32[8,1,128]{2,1,0:T(1,128)S(1)}, u32[]{:S(2)}, u32[]{:S(2)}) collective-permute-start(f32[8,1,128]{2,1,0:T(1,128)S(1)} %get-tuple-element.103), channel_id=1, source_target_pairs={{0,16},{16,32},{32,48},{48,64},{64,80},{80,96},{96,112},{1,17},{17... | collective-permute-start | bytes 12296 | tf_op jit(solution)/shard_map/ppermute | solution.py:23
  197.4 7.3 %collective-permute-start.6 = (f32[8,34,1]{2,1,0:T(8,128)S(1)}, f32[8,34,1]{2,1,0:T(8,128)S(1)}, u32[]{:S(2)}, u32[]{:S(2)}) collective-permute-start(f32[8,34,1]{2,1,0:T(8,128)S(1)} %get-tuple-element.95), channel_id=1, source_target_pairs={{1,0},{2,1},{3,2},{4,3},{5,4},{6,5},{7,6},{8,7},{9,8},{10,9},{11,1... | collective-permute-start | bytes 3272 | tf_op jit(solution)/shard_map/ppermute | solution.py:25
  201.9 9.3 %collective-permute-start.7 = (f32[8,34,1]{2,1,0:T(8,128)S(1)}, f32[8,34,1]{2,1,0:T(8,128)S(1)}, u32[]{:S(2)}, u32[]{:S(2)}) collective-permute-start(f32[8,34,1]{2,1,0:T(8,128)S(1)} %get-tuple-element.96), channel_id=1, source_target_pairs={{0,1},{1,2},{2,3},{3,4},{4,5},{5,6},{6,7},{7,8},{8,9},{9,10},{10,1... | collective-permute-start | bytes 3272 | tf_op jit(solution)/shard_map/ppermute | solution.py:23
  211.4 4.3 %collective-permute-start.8 = (f32[8,1,128]{2,1,0:T(1,128)S(1)}, f32[8,1,128]{2,1,0:T(1,128)S(1)}, u32[]{:S(2)}, u32[]{:S(2)}) collective-permute-start(f32[8,1,128]{2,1,0:T(1,128)S(1)} %get-tuple-element.102), channel_id=1, source_target_pairs={{16,0},{32,16},{48,32},{64,48},{80,64},{96,80},{112,96},{17,1},{33... | collective-permute-start | bytes 12296 | tf_op jit(solution)/shard_map/ppermute | solution.py:25
  213.3 4.9 %collective-permute-start.9 = (f32[8,1,128]{2,1,0:T(1,128)S(1)}, f32[8,1,128]{2,1,0:T(1,128)S(1)}, u32[]{:S(2)}, u32[]{:S(2)}) collective-permute-start(f32[8,1,128]{2,1,0:T(1,128)S(1)} %get-tuple-element.101), channel_id=1, source_target_pairs={{0,16},{16,32},{32,48},{48,64},{64,80},{80,96},{96,112},{1,17},{17... | collective-permute-start | bytes 12296 | tf_op jit(solution)/shard_map/ppermute | solution.py:23
  218.4 7.2 %collective-permute-start.10 = (f32[8,34,1]{2,1,0:T(8,128)S(1)}, f32[8,34,1]{2,1,0:T(8,128)S(1)}, u32[]{:S(2)}, u32[]{:S(2)}) collective-permute-start(f32[8,34,1]{2,1,0:T(8,128)S(1)} %get-tuple-element.93), channel_id=1, source_target_pairs={{1,0},{2,1},{3,2},{4,3},{5,4},{6,5},{7,6},{8,7},{9,8},{10,9},{11,1... | collective-permute-start | bytes 3272 | tf_op jit(solution)/shard_map/ppermute | solution.py:25
  220.3 9.3 %collective-permute-start.11 = (f32[8,34,1]{2,1,0:T(8,128)S(1)}, f32[8,34,1]{2,1,0:T(8,128)S(1)}, u32[]{:S(2)}, u32[]{:S(2)}) collective-permute-start(f32[8,34,1]{2,1,0:T(8,128)S(1)} %get-tuple-element.94), channel_id=1, source_target_pairs={{0,1},{1,2},{2,3},{3,4},{4,5},{5,6},{6,7},{7,8},{8,9},{9,10},{10,1... | collective-permute-start | bytes 3272 | tf_op jit(solution)/shard_map/ppermute | solution.py:23
  229.9 4.3 %collective-permute-start.12 = (f32[8,1,128]{2,1,0:T(1,128)S(1)}, f32[8,1,128]{2,1,0:T(1,128)S(1)}, u32[]{:S(2)}, u32[]{:S(2)}) collective-permute-start(f32[8,1,128]{2,1,0:T(1,128)S(1)} %get-tuple-element.100), channel_id=1, source_target_pairs={{16,0},{32,16},{48,32},{64,48},{80,64},{96,80},{112,96},{17,1},{33... | collective-permute-start | bytes 12296 | tf_op jit(solution)/shard_map/ppermute | solution.py:25
  232.0 4.9 %collective-permute-start.13 = (f32[8,1,128]{2,1,0:T(1,128)S(1)}, f32[8,1,128]{2,1,0:T(1,128)S(1)}, u32[]{:S(2)}, u32[]{:S(2)}) collective-permute-start(f32[8,1,128]{2,1,0:T(1,128)S(1)} %get-tuple-element.99), channel_id=1, source_target_pairs={{0,16},{16,32},{32,48},{48,64},{64,80},{80,96},{96,112},{1,17},{17... | collective-permute-start | bytes 12296 | tf_op jit(solution)/shard_map/ppermute | solution.py:23
  237.1 7.2 %collective-permute-start.14 = (f32[8,34,1]{2,1,0:T(8,128)S(1)}, f32[8,34,1]{2,1,0:T(8,128)S(1)}, u32[]{:S(2)}, u32[]{:S(2)}) collective-permute-start(f32[8,34,1]{2,1,0:T(8,128)S(1)} %get-tuple-element.91), channel_id=1, source_target_pairs={{1,0},{2,1},{3,2},{4,3},{5,4},{6,5},{7,6},{8,7},{9,8},{10,9},{11,1... | collective-permute-start | bytes 3272 | tf_op jit(solution)/shard_map/ppermute | solution.py:25
  239.0 9.3 %collective-permute-start.15 = (f32[8,34,1]{2,1,0:T(8,128)S(1)}, f32[8,34,1]{2,1,0:T(8,128)S(1)}, u32[]{:S(2)}, u32[]{:S(2)}) collective-permute-start(f32[8,34,1]{2,1,0:T(8,128)S(1)} %get-tuple-element.92), channel_id=1, source_target_pairs={{0,1},{1,2},{2,3},{3,4},{4,5},{5,6},{6,7},{7,8},{8,9},{9,10},{10,1... | collective-permute-start | bytes 3272 | tf_op jit(solution)/shard_map/ppermute | solution.py:23
  248.5 4.3 %collective-permute-start.16 = (f32[8,1,128]{2,1,0:T(1,128)S(1)}, f32[8,1,128]{2,1,0:T(1,128)S(1)}, u32[]{:S(2)}, u32[]{:S(2)}) collective-permute-start(f32[8,1,128]{2,1,0:T(1,128)S(1)} %get-tuple-element.98), channel_id=1, source_target_pairs={{16,0},{32,16},{48,32},{64,48},{80,64},{96,80},{112,96},{17,1},{33... | collective-permute-start | bytes 12296 | tf_op jit(solution)/shard_map/ppermute | solution.py:25
  250.5 4.9 %collective-permute-start.17 = (f32[8,1,128]{2,1,0:T(1,128)S(1)}, f32[8,1,128]{2,1,0:T(1,128)S(1)}, u32[]{:S(2)}, u32[]{:S(2)}) collective-permute-start(f32[8,1,128]{2,1,0:T(1,128)S(1)} %get-tuple-element.97), channel_id=1, source_target_pairs={{0,16},{16,32},{32,48},{48,64},{64,80},{80,96},{96,112},{1,17},{17... | collective-permute-start | bytes 12296 | tf_op jit(solution)/shard_map/ppermute | solution.py:23
  255.6 7.2 %collective-permute-start.18 = (f32[8,34,1]{2,1,0:T(8,128)S(1)}, f32[8,34,1]{2,1,0:T(8,128)S(1)}, u32[]{:S(2)}, u32[]{:S(2)}) collective-permute-start(f32[8,34,1]{2,1,0:T(8,128)S(1)} %get-tuple-element.89), channel_id=1, source_target_pairs={{1,0},{2,1},{3,2},{4,3},{5,4},{6,5},{7,6},{8,7},{9,8},{10,9},{11,1... | collective-permute-start | bytes 3272 | tf_op jit(solution)/shard_map/ppermute | solution.py:25
  257.5 9.3 %collective-permute-start.19 = (f32[8,34,1]{2,1,0:T(8,128)S(1)}, f32[8,34,1]{2,1,0:T(8,128)S(1)}, u32[]{:S(2)}, u32[]{:S(2)}) collective-permute-start(f32[8,34,1]{2,1,0:T(8,128)S(1)} %get-tuple-element.90), channel_id=1, source_target_pairs={{0,1},{1,2},{2,3},{3,4},{4,5},{5,6},{6,7},{7,8},{8,9},{9,10},{10,1... | collective-permute-start | bytes 3272 | tf_op jit(solution)/shard_map/ppermute | solution.py:23
where the time goes:
time: 269 us; the launch traced here: 268 us
  waiting for transfers between devices  84 us (31%)
  local copies, waits for them, and re-layouts  73.3 us (27%)
  starting transfers between devices  66.2 us (25%)
  matrix products  32.5 us (12%)
  other arithmetic  11 us (4%)
    all_to_all x1, waiting for transfers between devices, local(): lax.all_to_all(outgoing, ('gx', 'gy'), split_axis=0, concat_axis=0, tiled...  39 us
    ppermute x10, waiting for transfers between devices, extended(): lax.ppermute(tail, axis, [(i, (i + 1) % count) for i in range(ends)])  33.4 us
    gather x8, local copies, waits for them, and re-layouts, block_products(): bank_part = remap_bank[jnp.maximum(weight_ids, 0)]  32 us
    dot_general x8, matrix products, block_products(): jnp.einsum('gkfc,gkco->gfo', source_part, bank_part, preferred_element_ty...  30.8 us
    ppermute x10, starting transfers between devices, extended(): lax.ppermute(tail, axis, [(i, (i + 1) % count) for i in range(ends)])  23.6 us
    ppermute x10, starting transfers between devices, extended(): lax.ppermute(head, axis, [((i + 1) % count, i) for i in range(ends)])  21.6 us
    scatter x1, local copies, waits for them, and re-layouts, local(): jnp.zeros((slot_count,) + picked.shape[1:], jnp.bfloat16).at[slot_of]  15.6 us
    all_to_all x1, starting transfers between devices, local(): lax.all_to_all(labels, ('gx', 'gy'), split_axis=0, concat_axis=0, tiled=T...  12 us
  transfers between devices with their start and end apart: 22, of which 15 were waited for; matrix products, arithmetic and copies ran while one was open for 17% of the time, Pallas kernels for 0%

commit v1 on v0

v1 whole, which is shorter than its diff:
```python
import jax
import jax.numpy as jnp
from jax import lax
from jax.experimental import pallas as pl
from jax.experimental.pallas import tpu as pltpu
from jax.sharding import PartitionSpec as P

F = 8
AXD, AYD = 64, 256
OXD, OYD = 32, 128
NWB = 16
RECS = 128
SWEEPS = 4
OWNERS = 128
NGX, NGY = 8, 16
(W, T8, OWN, SLOT, DX, DY, DC, MX, MY, MC, SHIFT, PO, PX, PY, VO, VX, VY, POS) = range(18)
ABSENT = 256.0


def lanes(shape):
    return lax.broadcasted_iota(jnp.int32, shape, 1)


def swap_blocks(v):
    block = lanes((8, 128)) // 16
    for s in range(3):
        d = 1 << s
        high = (block & d) != 0
        n = list(v)
        for p in range(8):
            if not p & d:
                a, b = v[p], v[p | d]
                n[p] = jnp.where(high, pltpu.roll(b, 16 * d, 1), a)
                n[p | d] = jnp.where(high, b, pltpu.roll(a, 128 - 16 * d, 1))
        v = n
    return v


def send_kernel(tab, flux_in, above, below, before, after, diff, bank, out, lhs, prod, stage, mask, flux, sems):
    copies = [pltpu.make_async_copy(flux_in.at[:, pl.ds(g * 128, 128)], flux.at[g], sems.at[g]) for g in range(2)]
    for copy in copies:
        copy.start()
    lane = lanes((8, 128))
    sub = lax.broadcasted_iota(jnp.int32, (8, 128), 0)
    a_of, b_of = lane // 16, lane % 16

    is_label = (a_of == 2) & (b_of >= 4) & (b_of < 12) | (a_of == 3) & (b_of >= 4) & (b_of < 6)
    empty = jnp.where(is_label, ABSENT, 0.0).astype(jnp.float32)
    zero = jnp.zeros((8, 128), jnp.float32)

    def clear(o, carry):
        for j in range(3):
            stage[o, j, 0:8, :] = zero
            stage[o, j, 8:16, :] = empty if j == 2 else zero
        return carry

    lax.fori_loop(0, OWNERS + 1, clear, 0, unroll=3)

    def put_mask(at, cond):
        mask[at] = cond.astype(jnp.float32)

    put_mask(0, lane < 64)
    put_mask(1, lane >= 64)
    put_mask(2, b_of < 4)
    put_mask(3, (b_of >= 4) & (b_of < 8))
    put_mask(4, b_of >= 12)
    put_mask(5, (b_of >= 8) & (b_of < 12))
    put_mask(6, (lane < 64) & (b_of < 4))
    put_mask(7, (lane < 64) & (b_of >= 12))
    put_mask(8, (lane >= 64) & (b_of < 4))
    put_mask(9, (lane >= 64) & (b_of >= 12))

    wide = lanes((8, 256))
    left, right = before[0:8, :], after[0:8, :]

    def row(i):
        if i < 0:
            return jnp.concatenate([above[0:8, :], above[8:16, :]], axis=1)
        if i >= AXD:
            return jnp.concatenate([below[0:8, :], below[8:16, :]], axis=1)
        return jnp.concatenate([flux[g, pl.ds(i, 8, stride=AXD), :] for g in range(2)], axis=1)

    for copy in copies:
        copy.wait()
    for ti in range(4):
        x = [row(i) for i in range(ti * 16 - 1, ti * 16 + 17)]
        for k in range(3):
            vals = []
            for a in range(16):
                i = ti * 16 + a
                if k == 0:
                    vals.append(x[a + 1])
                elif k == 1:
                    vals.append((x[a + 2] - x[a]) * 0.5)
                else:
                    nxt = jnp.where(wide == 255, right[:, i : i + 1], pltpu.roll(x[a + 1], 255, 1))
                    prv = jnp.where(wide == 0, left[:, i : i + 1], pltpu.roll(x[a + 1], 1, 1))
                    vals.append((nxt - prv) * 0.5)
            for h in range(2):
                y = [swap_blocks([vals[h * 8 + q][:, g * 128 : (g + 1) * 128] for q in range(8)]) for g in range(2)]
                for q in range(8):
                    lhs[pl.ds((ti * 8 + q) * 16, 16), pl.ds(k * 256 + h * 128, 128)] = jnp.concatenate(
                        [y[0][q], y[1][q]], axis=0
                    ).astype(jnp.bfloat16)

    def product(n, carry):
        rhs = jnp.concatenate([bank[2 * n], bank[2 * n + 1]], axis=1)
        res = jnp.dot(lhs[...], rhs, preferred_element_type=jnp.float32)
        prod[2 * n] = res[:, :128]
        prod[2 * n + 1] = res[:, 128:]
        return carry

    lax.fori_loop(0, NWB // 2, product, 0)

    def record(r, carry):
        c8 = pl.multiple_of(tab[SLOT, r] * 8, 8)
        own, dx, dy, dc = tab[OWN, r], tab[DX, r], tab[DY, r], tab[DC, r]
        value = prod[tab[W, r], pl.ds(pl.multiple_of(tab[T8, r], 8), 8), :]
        stage[own, 0, pl.ds(c8, 8), :] = value
        stage[dx, 1, pl.ds(c8, 8), :] = jnp.where(mask[tab[MX, r]] > 0, value, stage[dx, 1, pl.ds(c8, 8), :])
        turned = pltpu.roll(value, tab[SHIFT, r], 1)
        stage[dy, 2, 0:8, :] = jnp.where(mask[tab[MY, r]] > 0, turned, stage[dy, 2, 0:8, :])
        stage[own, 2, 8:16, :] = jnp.where(lane == tab[PO, r], (sub + tab[VO, r]).astype(jnp.float32), stage[own, 2, 8:16, :])
        stage[dx, 2, 8:16, :] = jnp.where(lane == tab[PX, r], (sub + tab[VX, r]).astype(jnp.float32), stage[dx, 2, 8:16, :])
        stage[dy, 2, 8:16, :] = jnp.where(lane == tab[PY, r], (sub + tab[VY, r]).astype(jnp.float32), stage[dy, 2, 8:16, :])
        stage[dc, 2, 8:16, :] = stage[dc, 2, 8:16, :] + jnp.where(mask[tab[MC, r]] > 0, value, 0.0)
        return carry

    lax.fori_loop(0, RECS, record, 0, unroll=4)

    for at, rows, is_left in ((0, 0, True), (1, 0, False), (2, 24, True), (3, 24, False)):
        cells = diff[rows : rows + 8, :]
        high = cells.astype(jnp.bfloat16).astype(jnp.float32)
        low = cells - high
        d = tab[POS, at]
        old = stage[d, 2, 8:16, :]
        if is_left:
            new = jnp.where((lane >= 4) & (lane < 8), pltpu.roll(high, 4, 1), old)
            new = jnp.where((lane >= 8) & (lane < 12), pltpu.roll(low, 8, 1), new)
        else:
            new = jnp.where((lane >= 120) & (lane < 124), pltpu.roll(high, 124, 1), old)
            new = jnp.where((lane >= 116) & (lane < 120), pltpu.roll(low, 120, 1), new)
        stage[d, 2, 8:16, :] = new

    def convert(q, carry):
        out[pl.ds(q * 8, 8)] = stage[pl.ds(q * 8, 8)].astype(jnp.bfloat16)
        return carry

    lax.fori_loop(0, OWNERS // 8, convert, 0)


def ocean_kernel(tab, recv, diff, above, below, before, after, out, onehot, dext, u0, u1):
    lane = lanes((8, 128))
    a_of, b_of = lane // 16, lane % 16
    K = OWNERS * 16
    own_in = recv[:, 0].reshape(K, 128)
    pair_in = recv[:, 1].reshape(K, 128)
    side_in = recv[:, 2].reshape(K, 128)

    pick_row = lax.broadcasted_iota(jnp.int32, (16, 128), 0)
    pick_lane = lanes((16, 128))
    label_lane = jnp.where(pick_row < 8, 36 + pick_row, 44 + pick_row)
    pick = ((label_lane == pick_lane) & (pick_row < 10)).astype(jnp.float32).astype(jnp.bfloat16)
    keys = lax.dot_general(pick, side_in, (((1,), (1,)), ((), ())), preferred_element_type=jnp.float32)
    early = pltpu.roll(keys, K - 8, 1)
    klane = lanes((8, K))
    sub = lax.broadcasted_iota(jnp.int32, (8, K), 0).astype(jnp.float32)
    late = (klane & 8) != 0

    def spread(rows, at):
        return jnp.broadcast_to(rows[at : at + 1, :], (8, K))

    def both(at):
        return jnp.where(late, spread(keys, at + 1), spread(early, at)) - sub

    def first(at):
        return jnp.where(late, -1000.0, spread(early, at)) - sub

    def hot(base, key, count):
        for t in range(0, count, 2):
            pair = [jnp.where(key == 8.0 * (t + q), 1.0, 0.0) for q in range(2)]
            onehot[pl.ds(base + t * 8, 16), :] = jnp.concatenate(pair, axis=0).astype(jnp.bfloat16)

    hot(0, both(0), 32)
    hot(256, both(2), 8)
    hot(320, both(4), 8)
    hot(384, first(6), 4)
    hot(416, first(7), 4)
    hot(448, first(8), 4)
    hot(480, first(9), 4)
    hot(512, jnp.where(late, (klane & 7).astype(jnp.float32), -1000.0) - sub, 2)

    def dot(lo, hi, rhs):
        return jnp.dot(onehot[lo:hi, :], rhs, preferred_element_type=jnp.float32)

    own = dot(0, 256, own_in)
    pairs = dot(256, 384, pair_in)
    sides = dot(384, 528, side_in)

    def tile(x, at):
        return x[at * 8 : at * 8 + 8, :]

    def put_side(cells, rows):
        for a, e in rows:
            right = pltpu.roll(cells, (128 - 16 * a) % 128, 1)
            left = pltpu.roll(cells, (112 - 16 * a) % 128, 1)
            u0[e, :, 128:256] = jnp.where(lane < 4, right, jnp.where(lane >= 124, left, 0.0))

    for tx in range(4):
        rows = swap_blocks([tile(own, tx * 8 + ty) for ty in range(8)])
        for a in range(8):
            u0[4 + tx * 8 + a, :, 0:128] = rows[a]
        r = tile(sides, tx) + pltpu.roll(tile(sides, 4 + tx), 124, 1)
        l = tile(sides, 8 + tx) + pltpu.roll(tile(sides, 12 + tx), 4, 1)
        put_side(jnp.where(b_of < 4, r, l), [(a, 4 + tx * 8 + a) for a in range(8)])
    rows = swap_blocks([tile(pairs, ty) for ty in range(8)])
    for a in range(4):
        u0[36 + a, :, 0:128] = rows[a]
    rows = swap_blocks([tile(pairs, 8 + ty) for ty in range(8)])
    for a in range(4, 8):
        u0[a - 4, :, 0:128] = rows[a]
    put_side(tile(sides, 16), [(a, 36 + a) for a in range(4)] + [(a, a - 4) for a in range(4, 8)])

    def flag(at):
        return tab[POS, at].astype(jnp.float32)

    def corner(at):
        s = tab[POS, at]
        z = recv[jnp.minimum(s, OWNERS - 1), 2].astype(jnp.float32)[8:16, :]
        z = jnp.where(s < OWNERS, z, 0.0)
        left = pltpu.roll(z, 4, 1) + pltpu.roll(z, 8, 1)
        right = pltpu.roll(z, 124, 1) + pltpu.roll(z, 120, 1)
        return left if at % 2 == 0 else right

    def ends(left, right):
        return jnp.where(lane < 4, right, jnp.where(lane >= 124, left, 0.0))

    dext[0:8, 0:128] = above[40:48, :] * flag(4)
    dext[40:48, 0:128] = below[16:24, :] * flag(5)
    dext[8:40, 0:128] = diff[...]
    dext[0:8, 128:256] = ends(corner(0), corner(1))
    dext[40:48, 128:256] = ends(corner(2), corner(3))
    for q in range(4):
        dext[8 + q * 8 : 16 + q * 8, 128:256] = ends(
            before[8 + q * 8 : 16 + q * 8, :] * flag(6), after[8 + q * 8 : 16 + q * 8, :] * flag(7)
        )

    src, dst = u0, u1
    for sweep in range(SWEEPS):
        for e in range(sweep + 1, 39 - sweep):
            u = src[e]
            beside = src[e + 1] + src[e - 1] + pltpu.roll(u, 255, 1) + pltpu.roll(u, 1, 1)
            d = jnp.broadcast_to(dext[e + 4 : e + 5, :], (8, 256))
            new = u + d * (beside - 4.0 * u)
            if sweep < SWEEPS - 1:
                dst[e] = new
            else:
                out[pl.ds(e - 4, 8, stride=OXD), :] = new[:, :128]
        src, dst = dst, src


def record_table(owner, source, target, weight):
    gx, gy = lax.axis_index("gx"), lax.axis_index("gy")
    me = gx * NGY + gy
    ids = jnp.arange(RECS, dtype=jnp.int32)
    earlier = (owner[:, None] == owner[None, :]) & (ids[None, :] < ids[:, None])
    slot = jnp.sum(earlier.astype(jnp.int32), axis=1)
    ox, oy = owner // NGY, owner % NGY
    tx, ty = target // 8, target % 8
    sx = jnp.where(tx == 0, -1, jnp.where(tx == 3, 1, 0))
    sy = jnp.where(ty == 0, -1, jnp.where(ty == 7, 1, 0))
    ok_x = (sx != 0) & (ox + sx >= 0) & (ox + sx < NGX)
    ok_y = (sy != 0) & (oy + sy >= 0) & (oy + sy < NGY)
    dx = jnp.where(ok_x, owner + sx * NGY, OWNERS)
    dy = jnp.where(ok_y, owner + sy, OWNERS)
    dc = jnp.where(ok_x & ok_y, owner + sx * NGY + sy, OWNERS)
    kx = (tx == 3).astype(jnp.int32)
    ky = (ty == 7).astype(jnp.int32)
    ti, tj = source // 16, source % 16
    t8 = (ti * 16 + (tj % 8) * 2 + tj // 8) * 8

    def near(du, dv):
        ok = (gx + du >= 0) & (gx + du < NGX) & (gy + dv >= 0) & (gy + dv < NGY)
        return jnp.where(ok, me + du * NGY + dv, OWNERS)

    at = ids
    flags = [near(-1, -1), near(-1, 1), near(1, -1), near(1, 1), gx > 0, gx < NGX - 1, gy > 0, gy < NGY - 1]
    pos = jnp.zeros((RECS,), jnp.int32)
    for n, value in enumerate(flags):
        pos = jnp.where(at == n, value.astype(jnp.int32), pos)
    rows = [
        weight, t8, owner, slot, dx, dy, dc, kx, 2 + ky * 2 + slot, 6 + kx * 2 + ky,
        jnp.where(ky == 0, 4 * slot, (128 - 4 * slot) % 128),
        36 + slot, 38 + 2 * kx + slot, jnp.where(ky == 0, 42, 52) + slot,
        target * 8, ty * 8, tx * 8, pos,
    ]
    return jnp.stack(rows)


def local(flux, diffusivity, remap_bank, rec_owner, rec_source, rec_target, rec_weight):
    tab = record_table(rec_owner, rec_source, rec_target, rec_weight)

    def gx_message(i):
        return jnp.concatenate([flux[:, i, :128], flux[:, i, 128:], diffusivity], axis=0)

    def gy_message(j):
        return jnp.concatenate([jnp.pad(flux[:, :, j], ((0, 0), (0, 64))), diffusivity], axis=0)

    def shift(x, axis, count, by):
        return lax.ppermute(x, axis, [(i, (i + by) % count) for i in range(count)])

    above = shift(gx_message(AXD - 1), "gx", NGX, 1)
    below = shift(gx_message(0), "gx", NGX, -1)
    before = shift(gy_message(AYD - 1), "gy", NGY, 1)
    after = shift(gy_message(0), "gy", NGY, -1)

    vmem = pl.BlockSpec(memory_space=pltpu.VMEM)
    smem = pl.BlockSpec(memory_space=pltpu.SMEM)
    outgoing = pl.pallas_call(
        send_kernel,
        out_shape=jax.ShapeDtypeStruct((OWNERS, 3, 16, 128), jnp.bfloat16),
        in_specs=[smem, pl.BlockSpec(memory_space=pl.ANY)] + [vmem] * 6,
        out_specs=vmem,
        scratch_shapes=[
            pltpu.VMEM((512, 768), jnp.bfloat16),
            pltpu.VMEM((NWB, 512, 128), jnp.float32),
            pltpu.VMEM((OWNERS + 1, 3, 16, 128), jnp.float32),
            pltpu.VMEM((10, 8, 128), jnp.float32),
            pltpu.VMEM((2, F * AXD, 128), jnp.float32),
            pltpu.SemaphoreType.DMA((2,)),
        ],
        name="remap_send",
    )(tab, flux.reshape(F * AXD, AYD), above, below, before, after, diffusivity, remap_bank.reshape(NWB, 768, 128))
    arrived = lax.all_to_all(outgoing, ("gx", "gy"), split_axis=0, concat_axis=0, tiled=True)
    ocean = pl.pallas_call(
        ocean_kernel,
        out_shape=jax.ShapeDtypeStruct((F * OXD, OYD), jnp.float32),
        in_specs=[smem] + [vmem] * 6,
        out_specs=vmem,
        scratch_shapes=[
            pltpu.VMEM((528, OWNERS * 16), jnp.bfloat16),
            pltpu.VMEM((48, 256), jnp.float32),
            pltpu.VMEM((40, 8, 256), jnp.float32),
            pltpu.VMEM((40, 8, 256), jnp.float32),
        ],
        name="ocean",
    )(tab, arrived, diffusivity, above, below, before, after)
    return ocean.reshape(F, OXD, OYD)


def solution(mesh):
    in_specs = (
        P(None, "gx", "gy"),
        P("gx", "gy"),
        P(),
        P(("gx", "gy")),
        P(("gx", "gy")),
        P(("gx", "gy")),
        P(("gx", "gy")),
    )
    return jax.shard_map(local, mesh=mesh, in_specs=in_specs, out_specs=P(None, "gx", "gy"), check_vma=False)
```

time: 269 us -> 72.9 us (0.27)
  the two profiles are of different devices: /device:TPU:10 before, /device:TPU:0 now
where the time goes in v1:
time: 72.9 us; the launch traced here: 72.5 us
  blocking collectives  30.1 us (41%)
  Pallas kernels  22.7 us (31%)
  starting transfers between devices  8.87 us (12%)
  waiting for transfers between devices  4.92 us (7%)
  local copies, waits for them, and re-layouts  4.77 us (7%)
  other arithmetic  0.99 us (1%)
    all_to_all x1, blocking collectives, local(): lax.all_to_all(outgoing, ('gx', 'gy'), split_axis=0, concat_axis=0, tiled...  30.1 us
    pallas_call x1, Pallas kernels, local(): pl.pallas_call(send_kernel, out_shape=jax.ShapeDtypeStruct((OWNERS, 3, 16...  18.8 us
    ppermute x4, starting transfers between devices, shift(): return lax.ppermute(x, axis, [(i, (i + by) % count) for i in range(count)])  8.87 us
    ppermute x4, waiting for transfers between devices, shift(): return lax.ppermute(x, axis, [(i, (i + by) % count) for i in range(count)])  4.92 us
    pallas_call x1, Pallas kernels, local(): pl.pallas_call(ocean_kernel, out_shape=jax.ShapeDtypeStruct((F * OXD, OYD...  3.88 us
    another operation x1, local copies, waits for them, and re-layouts, record_table(): return jnp.stack(rows)  1.83 us
  transfers between devices with their start and end apart: 4, of which 1 were waited for; matrix products, arithmetic and copies ran while one was open for 5% of the time, Pallas kernels for 0%

profile of v1, /device:TPU:0, one launch (start us, length us, event | category | flops | bytes accessed | tf_op | source)
XLA Modules:
  0.0 72.5 jit_solution(14477967718785382228)
XLA Ops:
  0.0 0.0 copy-start
  0.0 0.0 copy-start.5
  0.0 0.0 copy-start.7
  0.0 0.0 copy-start.8
  0.0 0.0 copy-start.6
  0.0 0.9 %fusion.11 = (f32[8,1,128]{2,1,0:T(1,128)S(1)}, f32[8,1,128]{2,1,0:T(1,128)S(1)}, f32[8,1,128]{2,1,0:T(1,128)S(1)}, f32[8,1,128]{2,1,0:T(1,128)S(1)}) fusion(f32[8,64,256]{2,1,0:T(8,128)} %param.7), kind=kLoop, calls=%fused_computation.70 | loop fusion | bytes 32768 | tf_op jit(solution)/shard_map/slice | solution.py:304
  0.9 0.7 %pad_maximum_fusion = (f32[48,128]{1,0:T(8,128)S(1)}, f32[48,128]{1,0:T(8,128)S(1)}) fusion(f32[32,128]{1,0:T(8,128)} %diff.3, f32[8,128]{1,0:T(8,128)S(1)} %bitcast.52, f32[8,128]{1,0:T(8,128)S(1)} %bitcast.51, f32[8,128]{1,0:T(8,128)S(1)} %bitcast.53, f32[8,128]{1,0:T(8,128)S(1)} %bitcast.54), kind=kLoop, calls=%fused_computation.3 | loop fusion | flops 24576 | bytes 81920 | tf_op jit(solution)/shard_map/concatenate | solution.py:304
  1.6 2.3 %collective-permute-start.1 = (f32[48,128]{1,0:T(8,128)S(1)}, f32[48,128]{1,0:T(8,128)S(1)}, u32[]{:S(2)}, u32[]{:S(2)}) collective-permute-start(f32[48,128]{1,0:T(8,128)S(1)} %get-tuple-element.20), channel_id=1, source_target_pairs={{0,112},{16,0},{32,16},{48,32},{64,48},{80,64},{96,80},{112,96},{1... | collective-permute-start | bytes 73736 | tf_op jit(solution)/shard_map/ppermute | solution.py:310
  3.9 0.0 collective-permute-start
  3.9 1.2 %fusion.10 = (f32[8,64,1]{2,1,0:T(8,128)S(1)}, f32[8,64,1]{2,1,0:T(8,128)S(1)}) fusion(f32[8,64,256]{2,1,0:T(8,128)} %param.7), kind=kLoop, calls=%fused_computation.69 | loop fusion | bytes 8192 | tf_op jit(solution)/shard_map/slice | solution.py:307
  5.1 0.1 copy.25
  5.2 0.1 copy.24
  5.4 0.0 copy-done
  5.4 6.6 %collective-permute-start.3 = (f32[40,128]{1,0:T(8,128)S(1)}, f32[40,128]{1,0:T(8,128)S(1)}, u32[]{:S(2)}, u32[]{:S(2)}) collective-permute-start(f32[40,128]{1,0:T(8,128)S(1)} %get-tuple-element.18), channel_id=1, source_target_pairs={{0,15},{1,0},{2,1},{3,2},{4,3},{5,4},{6,5},{7,6},{8,7},{9,8},{10,9... | collective-permute-start | bytes 61448 | tf_op jit(solution)/shard_map/ppermute | solution.py:310
  11.9 0.0 collective-permute-start.2
  11.9 0.0 copy-done.5
  11.9 0.2 convert_reduce_fusion
  12.1 0.0 copy-done.7
  12.3 0.0 copy-done.8
  12.3 0.0 copy-done.6
  12.3 1.8 %stack.73.tab = s32[18,128]{1,0:T(8,128)} concatenate(s32[1,128]{1,0:T(1,128)S(1)} %bitcast.57, s32[1,128]{1,0:T(1,128)S(1)} %multiply_bitcast_fusion.3, s32[1,128]{1,0:T(1,128)S(1)} %bitcast.55, s32[1,128]{1,0:T(1,128)S(1)} %bitcast.56, s32[1,128]{1,0:T(1,128)S(1)} %get-tuple-element.33, s32[1,128]{1,0:T(1,128)S(1)} %get-tuple-element.32, s32[1,128]{1,0:T(1,128)S(1)} %get-tuple-element.28, ...), dimensions={0} | concatenate | bytes 18432 | tf_op jit(solution)/shard_map/stack | solution.py:297
  14.1 0.0 collective-permute-done.3.after
  14.1 0.0 copy-start.3
  14.1 4.9 %collective-permute-done.2.before = f32[40,128]{1,0:T(8,128)S(1)} collective-permute-done((f32[40,128]{1,0:T(8,128)S(1)}, f32[40,128]{1,0:T(8,128)S(1)}, u32[]{:S(2)}, u32[]{:S(2)}) %collective-permute-start.2) | collective-permute-done | bytes 20512 | tf_op jit(solution)/shard_map/ppermute | solution.py:310
  19.0 0.0 copy-start.4
  19.0 0.0 collective-permute-done.1.below
  19.1 0.0 copy-start.1
  19.1 0.0 collective-permute-done.above
  19.1 0.0 copy-start.2
  19.1 0.0 copy-done.3
  19.1 0.6 copy-done.4
  19.6 0.0 copy-done.1
  19.7 0.0 copy-done.2
  19.7 18.8 %remap_send.1 = bf16[128,3,16,128]{3,2,1,0:T(8,128)(2,1)} custom-call(s32[18,128]{1,0:T(8,128)} %stack.73.tab, f32[512,256]{1,0:T(8,128)} %bitcast.48, f32[48,128]{1,0:T(8,128)} %copy-done.2, f32[48,128]{1,0:T(8,128)} %copy-done.1, f32[40,128]{1,0:T(8,128)} %copy-done.4, f32[40,128]{1,0:T(8,128)} %copy-done.3, f32[32,128]{1,0:T(8,128)} %diff.3, ...), custom_call_target="tpu_custom_call" | custom-call | tf_op jit(solution)/shard_map/remap_send/pallas_call | solution.py:319
  38.5 30.1 %all_to_all.5.recv = bf16[128,3,16,128]{3,2,1,0:T(8,128)(2,1)} all-to-all(bf16[128,3,16,128]{3,2,1,0:T(8,128)(2,1)} %remap_send.1), channel_id=1, replica_groups=mesh['gx'=8,'gy'=16] {'gx','gy'}, dimensions={0} | all-to-all | bytes 3145728 | tf_op jit(solution)/shard_map/all_to_all | solution.py:334
  68.6 3.9 %ocean.1 = f32[256,128]{1,0:T(8,128)} custom-call(s32[18,128]{1,0:T(8,128)} %stack.73.tab, bf16[128,3,16,128]{3,2,1,0:T(8,128)(2,1)} %all_to_all.5.recv, f32[32,128]{1,0:T(8,128)} %diff.3, f32[48,128]{1,0:T(8,128)} %copy-done.2, f32[48,128]{1,0:T(8,128)} %copy-done.1, f32[40,128]{1,0:T(8,128)} %copy-done.4, f32[40,128]{1,0:T(8,128)} %copy-done.3), custom_call_target="tpu_custom_call" | custom-call | tf_op jit(solution)/shard_map/ocean/pallas_call | solution.py:335
  (7 shorter events, 0.1 us)
Async XLA Ops:
  0.0 5.4 %copy-start = (f32[32,128]{1,0:T(8,128)S(1)}, f32[32,128]{1,0:T(8,128)}, u32[]{:S(2)}) copy-start(f32[32,128]{1,0:T(8,128)} %diff.3) | copy-start | bytes 49156
  0.0 11.9 %copy-start.5 = (s32[128]{0:T(128)S(1)}, s32[128]{0:T(128)}, u32[]{:S(2)}) copy-start(s32[128]{0:T(128)} %param.10) | copy-start | bytes 1540
  0.0 12.1 %copy-start.7 = (s32[128]{0:T(128)S(1)}, s32[128]{0:T(128)}, u32[]{:S(2)}) copy-start(s32[128]{0:T(128)} %param.12) | copy-start | bytes 1540
  0.0 12.2 %copy-start.8 = (s32[128]{0:T(128)S(1)}, s32[128]{0:T(128)}, u32[]{:S(2)}) copy-start(s32[128]{0:T(128)} %param.11) | copy-start | bytes 1540
  0.0 12.3 %copy-start.6 = (s32[128]{0:T(128)S(1)}, s32[128]{0:T(128)}, u32[]{:S(2)}) copy-start(s32[128]{0:T(128)} %param.13) | copy-start | bytes 1540
  1.6 17.4 %collective-permute-start.1 = (f32[48,128]{1,0:T(8,128)S(1)}, f32[48,128]{1,0:T(8,128)S(1)}, u32[]{:S(2)}, u32[]{:S(2)}) collective-permute-start(f32[48,128]{1,0:T(8,128)S(1)} %get-tuple-element.20), channel_id=1, source_target_pairs={{0,112},{16,0},{32,16},{48,32},{64,48},{80,64},{96,80},{112,96},{1... | collective-permute-start | bytes 73736 | tf_op jit(solution)/shard_map/ppermute | solution.py:310
  3.9 15.1 %collective-permute-start = (f32[48,128]{1,0:T(8,128)S(1)}, f32[48,128]{1,0:T(8,128)S(1)}, u32[]{:S(2)}, u32[]{:S(2)}) collective-permute-start(f32[48,128]{1,0:T(8,128)S(1)} %get-tuple-element.21), channel_id=1, source_target_pairs={{0,16},{16,32},{32,48},{48,64},{64,80},{80,96},{96,112},{112,0},{1... | collective-permute-start | bytes 73736 | tf_op jit(solution)/shard_map/ppermute | solution.py:310
  5.4 8.7 %collective-permute-start.3 = (f32[40,128]{1,0:T(8,128)S(1)}, f32[40,128]{1,0:T(8,128)S(1)}, u32[]{:S(2)}, u32[]{:S(2)}) collective-permute-start(f32[40,128]{1,0:T(8,128)S(1)} %get-tuple-element.18), channel_id=1, source_target_pairs={{0,15},{1,0},{2,1},{3,2},{4,3},{5,4},{6,5},{7,6},{8,7},{9,8},{10,9... | collective-permute-start | bytes 61448 | tf_op jit(solution)/shard_map/ppermute | solution.py:310
  11.9 7.1 %collective-permute-start.2 = (f32[40,128]{1,0:T(8,128)S(1)}, f32[40,128]{1,0:T(8,128)S(1)}, u32[]{:S(2)}, u32[]{:S(2)}) collective-permute-start(f32[40,128]{1,0:T(8,128)S(1)} %get-tuple-element.19), channel_id=1, source_target_pairs={{0,1},{1,2},{2,3},{3,4},{4,5},{5,6},{6,7},{7,8},{8,9},{9,10},{10,1... | collective-permute-start | bytes 61448 | tf_op jit(solution)/shard_map/ppermute | solution.py:310
  14.1 4.9 %copy-start.3 = (f32[40,128]{1,0:T(8,128)}, f32[40,128]{1,0:T(8,128)S(1)}, u32[]{:S(2)}) copy-start(f32[40,128]{1,0:T(8,128)S(1)} %collective-permute-done.3.after) | copy-start | bytes 61444
  19.0 0.6 copy-start.4
  19.1 0.6 copy-start.1
  19.1 0.6 copy-start.2

commit v2 on v1

v2 whole, which is shorter than its diff:
```python
import jax
import jax.numpy as jnp
from jax import lax
from jax.experimental import pallas as pl
from jax.experimental.pallas import tpu as pltpu
from jax.sharding import PartitionSpec as P

F = 8
AXD, AYD = 64, 256
OXD, OYD = 32, 128
NWB = 16
RECS = 128
SWEEPS = 4
OWNERS = 128
NGX, NGY = 8, 16
(PROD, OWN, XROW, YROW, CROW, KX, YQ, CC, SHIFT, OWNER, XTO, YTO, PO, PX, PY, VO, VX, VY) = range(18)
TAB_ROWS = 24
ABSENT = 256.0
CORNERS = ((-1, -1), (-1, 1), (1, -1), (1, 1))


def lanes(shape):
    return lax.broadcasted_iota(jnp.int32, shape, 1)


def swap_blocks(v):
    block = lanes((8, 128)) // 16
    for s in range(3):
        d = 1 << s
        high = (block & d) != 0
        n = list(v)
        for p in range(8):
            if not p & d:
                a, b = v[p], v[p | d]
                n[p] = jnp.where(high, pltpu.roll(b, 16 * d, 1), a)
                n[p | d] = jnp.where(high, b, pltpu.roll(a, 128 - 16 * d, 1))
        v = n
    return v


def load_flux(flux_in, flux, sems):
    return [pltpu.make_async_copy(flux_in.at[:, pl.ds(g * 128, 128)], flux.at[g], sems.at[g]) for g in range(2)]


def neighbour(du, dv):
    gx, gy = lax.axis_index("gx") + du, lax.axis_index("gy") + dv
    return jnp.where((gx >= 0) & (gx < NGX) & (gy >= 0) & (gy < NGY), gx * NGY + gy, OWNERS)


def prepare_kernel(flux_in, diff, owner_in, source_in, target_in, weight_in, down, up, after, before, tab, flux, sems):
    copies = load_flux(flux_in, flux, sems)
    for copy in copies:
        copy.start()
    lane = lanes((8, 128))
    owner, source, target, weight = owner_in[...], source_in[...], target_in[...], weight_in[...]
    across = jnp.broadcast_to(owner, (RECS, RECS))
    along = jnp.transpose(across.astype(jnp.float32)).astype(jnp.int32)
    sub = lax.broadcasted_iota(jnp.int32, (RECS, RECS), 0)
    earlier = jnp.where((across == along) & (sub < lanes((RECS, RECS))), 1.0, 0.0)
    slot = jnp.sum(earlier, axis=0, keepdims=True).astype(jnp.int32)
    ox, oy = owner >> 4, owner & 15
    tx, ty = target >> 3, target & 7
    sx = jnp.where(tx == 0, -1, jnp.where(tx == 3, 1, 0))
    sy = jnp.where(ty == 0, -1, jnp.where(ty == 7, 1, 0))
    ok_x = (sx != 0) & (ox + sx >= 0) & (ox + sx < NGX)
    ok_y = (sy != 0) & (oy + sy >= 0) & (oy + sy < NGY)
    dx = jnp.where(ok_x, owner + sx * NGY, OWNERS)
    dy = jnp.where(ok_y, owner + sy, OWNERS)
    dc = jnp.where(ok_x & ok_y, owner + sx * NGY + sy, OWNERS)
    kx = jnp.where(tx == 3, 1, 0)
    ky = jnp.where(ty == 7, 1, 0)
    ti, tj = source >> 4, source & 15
    t8 = (ti * 16 + (tj & 7) * 2 + (tj >> 3)) * 8
    rows = [
        weight * 512 + t8, owner * 16 + slot * 8, dx * 16 + slot * 8, dy * 8, dc * 16 + slot * 8,
        kx, jnp.where(ky == 0, slot, 3 - slot), kx * 4 + ky * 3, jnp.where(ky == 0, 4 * slot, (128 - 4 * slot) & 127),
        owner, dx, dy, 36 + slot, 38 + 2 * kx + slot, jnp.where(ky == 0, 42, 52) + slot,
        target * 8 + 1, ty * 8 + 1, tx * 8 + 1,
    ]
    for n, value in enumerate(rows):
        tab[n : n + 1, :] = value
    for n in range(len(rows), TAB_ROWS):
        tab[n : n + 1, :] = slot

    for to in (down, up):
        to[16:48, :] = diff[...]
    for to in (after, before):
        to[8:40, :] = diff[...]
    for copy in copies:
        copy.wait()

    def row(i, g):
        return flux[g, pl.ds(i, 8, stride=AXD), :]

    for g in range(2):
        down[g * 8 : g * 8 + 8, :] = row(AXD - 1, g)
        up[g * 8 : g * 8 + 8, :] = row(0, g)
    last = jnp.zeros((8, 128), jnp.float32)
    first = jnp.zeros((8, 128), jnp.float32)
    for i in range(AXD):
        last = jnp.where(lane == i, row(i, 1)[:, 127:128], last)
        first = jnp.where(lane == i, row(i, 0)[:, 0:1], first)
    after[0:8, :] = last
    before[0:8, :] = first


def send_kernel(tab, tabv, flux_in, above, below, before, after, diff, bank, out, lhs, prod, owns, pairs, sides, corners, lab, flux, sems):
    copies = load_flux(flux_in, flux, sems)
    for copy in copies:
        copy.start()
    lane = lanes((8, 128))
    sub = lax.broadcasted_iota(jnp.int32, (8, 128), 0)
    a_of, b_of = lane // 16, lane % 16

    rows3 = lax.broadcasted_iota(jnp.int32, (128, 3 * RECS), 0)

    def three(*at):
        return jnp.concatenate([jnp.broadcast_to(tabv[n : n + 1, :], (128, RECS)) for n in at], axis=1)

    going = jnp.where(three(OWNER, XTO, YTO) == rows3, 1.0, 0.0).astype(jnp.bfloat16)
    label = jnp.where(three(PO, PX, PY) == rows3, three(VO, VX, VY), 0).astype(jnp.float32).astype(jnp.bfloat16)
    lab[...] = lax.dot_general(going, label, (((1,), (1,)), ((), ())), preferred_element_type=jnp.float32)
    is_label = (a_of == 2) & (b_of >= 4) & (b_of < 12) | (a_of == 3) & (b_of >= 4) & (b_of < 6)
    absent = jnp.where(is_label, ABSENT, 0.0)
    offset = (sub - 1).astype(jnp.float32)

    zero = jnp.zeros((8, 128), jnp.float32)

    def clear(o, carry):
        at = pl.multiple_of(o * 16, 16)
        half = pl.multiple_of(o * 8, 8)
        owns[pl.ds(at, 8), :] = zero
        owns[pl.ds(at + 8, 8), :] = zero
        pairs[pl.ds(at, 8), :] = zero
        pairs[pl.ds(at + 8, 8), :] = zero
        sides[pl.ds(half, 8), :] = zero
        corners[pl.ds(at, 8), :] = zero
        corners[pl.ds(at + 8, 8), :] = zero
        return carry

    lax.fori_loop(0, OWNERS, clear, 0, unroll=4)

    wide = lanes((8, 256))
    left, right = before[0:8, :], after[0:8, :]

    def row(i):
        if i < 0:
            return jnp.concatenate([above[0:8, :], above[8:16, :]], axis=1)
        if i >= AXD:
            return jnp.concatenate([below[0:8, :], below[8:16, :]], axis=1)
        return jnp.concatenate([flux[g, pl.ds(i, 8, stride=AXD), :] for g in range(2)], axis=1)

    for copy in copies:
        copy.wait()
    for ti in range(4):
        x = [row(i) for i in range(ti * 16 - 1, ti * 16 + 17)]
        for k in range(3):
            vals = []
            for a in range(16):
                i = ti * 16 + a
                if k == 0:
                    vals.append(x[a + 1])
                elif k == 1:
                    vals.append((x[a + 2] - x[a]) * 0.5)
                else:
                    nxt = jnp.where(wide == 255, right[:, i : i + 1], pltpu.roll(x[a + 1], 255, 1))
                    prv = jnp.where(wide == 0, left[:, i : i + 1], pltpu.roll(x[a + 1], 1, 1))
                    vals.append((nxt - prv) * 0.5)
            for h in range(2):
                y = [swap_blocks([vals[h * 8 + q][:, g * 128 : (g + 1) * 128] for q in range(8)]) for g in range(2)]
                for q in range(8):
                    lhs[pl.ds((ti * 8 + q) * 16, 16), pl.ds(k * 256 + h * 128, 128)] = jnp.concatenate(
                        [y[0][q], y[1][q]], axis=0
                    ).astype(jnp.bfloat16)

    def product(n, carry):
        rhs = jnp.concatenate([bank[2 * n], bank[2 * n + 1]], axis=1)
        res = jnp.dot(lhs[...], rhs, preferred_element_type=jnp.float32)
        at = pl.multiple_of(n * 1024, 1024)
        prod[pl.ds(at, 512), :] = res[:, :128]
        prod[pl.ds(at + 512, 512), :] = res[:, 128:]
        return carry

    lax.fori_loop(0, NWB // 2, product, 0)

    half_of, quarter_of = lane // 64, b_of // 4
    code = half_of * 4 + quarter_of

    def rows(ref, at):
        return ref.at[pl.ds(pl.multiple_of(at, 8), 8), :]

    for r in range(RECS):
        value = rows(prod, tab[PROD, r])[...]
        rows(owns, tab[OWN, r])[...] = value
        pltpu.store(rows(pairs, tab[XROW, r]), value, mask=half_of == tab[KX, r])
        pltpu.store(rows(sides, tab[YROW, r]), pltpu.roll(value, tab[SHIFT, r], 1), mask=quarter_of == tab[YQ, r])
        pltpu.store(rows(corners, tab[CROW, r]), value, mask=code == tab[CC, r])

    for du, dv in CORNERS:
        first = 0 if du < 0 else 24
        cells = diff[first : first + 8, :]
        high = cells.astype(jnp.bfloat16).astype(jnp.float32)
        low = cells - high
        to = rows(corners, neighbour(du, dv) * 16)
        if dv < 0:
            pltpu.store(to, pltpu.roll(high, 4, 1), mask=(lane >= 4) & (lane < 8))
            pltpu.store(to, pltpu.roll(low, 8, 1), mask=(lane >= 8) & (lane < 12))
        else:
            pltpu.store(to, pltpu.roll(high, 124, 1), mask=(lane >= 120) & (lane < 124))
            pltpu.store(to, pltpu.roll(low, 120, 1), mask=(lane >= 116) & (lane < 120))

    def convert(o, carry):
        at = pl.multiple_of(o * 16, 16)
        half = pl.ds(pl.multiple_of(o * 8, 8), 8)
        found = jnp.broadcast_to(lab[pl.ds(o, 1), :], (8, 128))
        tags = jnp.where(found > 0, found + offset, absent)
        last = tags + (corners[pl.ds(at, 8), :] + corners[pl.ds(at + 8, 8), :])
        out[o, 0] = owns[pl.ds(at, 16), :].astype(jnp.bfloat16)
        out[o, 1] = pairs[pl.ds(at, 16), :].astype(jnp.bfloat16)
        out[o, 2] = jnp.concatenate([sides[half, :], last], axis=0).astype(jnp.bfloat16)
        return carry

    lax.fori_loop(0, OWNERS, convert, 0, unroll=8)


def ocean_kernel(recv, diff, above, below, before, after, out, onehot, dext, u0, u1):
    lane = lanes((8, 128))
    a_of, b_of = lane // 16, lane % 16
    K = OWNERS * 16
    own_in = recv[:, 0].reshape(K, 128)
    pair_in = recv[:, 1].reshape(K, 128)
    side_in = recv[:, 2].reshape(K, 128)

    pick_row = lax.broadcasted_iota(jnp.int32, (16, 128), 0)
    pick_lane = lanes((16, 128))
    label_lane = jnp.where(pick_row < 8, 36 + pick_row, 44 + pick_row)
    pick = ((label_lane == pick_lane) & (pick_row < 10)).astype(jnp.float32).astype(jnp.bfloat16)
    keys = lax.dot_general(pick, side_in, (((1,), (1,)), ((), ())), preferred_element_type=jnp.float32)
    early = pltpu.roll(keys, K - 8, 1)
    klane = lanes((8, K))
    sub = lax.broadcasted_iota(jnp.int32, (8, K), 0).astype(jnp.float32)
    late = (klane & 8) != 0

    def spread(rows, at):
        return jnp.broadcast_to(rows[at : at + 1, :], (8, K))

    def both(at):
        return jnp.where(late, spread(keys, at + 1), spread(early, at)) - sub

    def first(at):
        return jnp.where(late, -1000.0, spread(early, at)) - sub

    def hot(base, key, count):
        for t in range(0, count, 2):
            pair = [jnp.where(key == 8.0 * (t + q), 1.0, 0.0) for q in range(2)]
            onehot[pl.ds(base + t * 8, 16), :] = jnp.concatenate(pair, axis=0).astype(jnp.bfloat16)

    hot(0, both(0), 32)
    hot(256, both(2), 8)
    hot(320, both(4), 8)
    hot(384, first(6), 4)
    hot(416, first(7), 4)
    hot(448, first(8), 4)
    hot(480, first(9), 4)
    hot(512, jnp.where(late, (klane & 7).astype(jnp.float32), -1000.0) - sub, 2)

    def dot(lo, hi, rhs):
        return jnp.dot(onehot[lo:hi, :], rhs, preferred_element_type=jnp.float32)

    own = dot(0, 256, own_in)
    pairs = dot(256, 384, pair_in)
    sides = dot(384, 528, side_in)

    def tile(x, at):
        return x[at * 8 : at * 8 + 8, :]

    def put_side(cells, rows):
        for a, e in rows:
            right = pltpu.roll(cells, (128 - 16 * a) % 128, 1)
            left = pltpu.roll(cells, (112 - 16 * a) % 128, 1)
            u0[e, :, 128:256] = jnp.where(lane < 4, right, jnp.where(lane >= 124, left, 0.0))

    for tx in range(4):
        rows = swap_blocks([tile(own, tx * 8 + ty) for ty in range(8)])
        for a in range(8):
            u0[4 + tx * 8 + a, :, 0:128] = rows[a]
        r = tile(sides, tx) + pltpu.roll(tile(sides, 4 + tx), 124, 1)
        l = tile(sides, 8 + tx) + pltpu.roll(tile(sides, 12 + tx), 4, 1)
        put_side(jnp.where(b_of < 4, r, l), [(a, 4 + tx * 8 + a) for a in range(8)])
    rows = swap_blocks([tile(pairs, ty) for ty in range(8)])
    for a in range(4):
        u0[36 + a, :, 0:128] = rows[a]
    rows = swap_blocks([tile(pairs, 8 + ty) for ty in range(8)])
    for a in range(4, 8):
        u0[a - 4, :, 0:128] = rows[a]
    put_side(tile(sides, 16), [(a, 36 + a) for a in range(4)] + [(a, a - 4) for a in range(4, 8)])

    def flag(du, dv):
        return jnp.where(neighbour(du, dv) < OWNERS, 1.0, 0.0)

    def corner(du, dv):
        s = neighbour(du, dv)
        z = recv[jnp.minimum(s, OWNERS - 1), 2].astype(jnp.float32)[8:16, :]
        z = jnp.where(s < OWNERS, z, 0.0)
        left = pltpu.roll(z, 4, 1) + pltpu.roll(z, 8, 1)
        right = pltpu.roll(z, 124, 1) + pltpu.roll(z, 120, 1)
        return left if dv < 0 else right

    def ends(left, right):
        return jnp.where(lane < 4, right, jnp.where(lane >= 124, left, 0.0))

    dext[0:8, 0:128] = above[40:48, :] * flag(-1, 0)
    dext[40:48, 0:128] = below[16:24, :] * flag(1, 0)
    dext[8:40, 0:128] = diff[...]
    dext[0:8, 128:256] = ends(corner(-1, -1), corner(-1, 1))
    dext[40:48, 128:256] = ends(corner(1, -1), corner(1, 1))
    for q in range(4):
        dext[8 + q * 8 : 16 + q * 8, 128:256] = ends(
            before[8 + q * 8 : 16 + q * 8, :] * flag(0, -1), after[8 + q * 8 : 16 + q * 8, :] * flag(0, 1)
        )

    src, dst = u0, u1
    for sweep in range(SWEEPS):
        for e in range(sweep + 1, 39 - sweep):
            u = src[e]
            beside = src[e + 1] + src[e - 1] + pltpu.roll(u, 255, 1) + pltpu.roll(u, 1, 1)
            d = jnp.broadcast_to(dext[e + 4 : e + 5, :], (8, 256))
            new = u + d * (beside - 4.0 * u)
            if sweep < SWEEPS - 1:
                dst[e] = new
            else:
                out[pl.ds(e - 4, 8, stride=OXD), :] = new[:, :128]
        src, dst = dst, src


def local(flux, diffusivity, remap_bank, rec_owner, rec_source, rec_target, rec_weight):
    vmem = pl.BlockSpec(memory_space=pltpu.VMEM)
    smem = pl.BlockSpec(memory_space=pltpu.SMEM)
    anywhere = pl.BlockSpec(memory_space=pl.ANY)
    flux_rows = flux.reshape(F * AXD, AYD)
    flux_scratch = [pltpu.VMEM((2, F * AXD, 128), jnp.float32), pltpu.SemaphoreType.DMA((2,))]
    records = [x.reshape(1, RECS) for x in (rec_owner, rec_source, rec_target, rec_weight)]
    f32, i32 = jnp.float32, jnp.int32
    down, up, right, left, tab = pl.pallas_call(
        prepare_kernel,
        out_shape=[jax.ShapeDtypeStruct((48, 128), f32)] * 2
        + [jax.ShapeDtypeStruct((40, 128), f32)] * 2
        + [jax.ShapeDtypeStruct((TAB_ROWS, RECS), i32)],
        in_specs=[anywhere] + [vmem] * 5,
        out_specs=[vmem] * 5,
        scratch_shapes=flux_scratch,
        name="prepare",
    )(flux_rows, diffusivity, *records)

    def shift(x, axis, count, by):
        return lax.ppermute(x, axis, [(i, (i + by) % count) for i in range(count)])

    above = shift(down, "gx", NGX, 1)
    below = shift(up, "gx", NGX, -1)
    before = shift(right, "gy", NGY, 1)
    after = shift(left, "gy", NGY, -1)

    outgoing = pl.pallas_call(
        send_kernel,
        out_shape=jax.ShapeDtypeStruct((OWNERS, 3, 16, 128), jnp.bfloat16),
        in_specs=[smem, vmem, anywhere] + [vmem] * 6,
        out_specs=vmem,
        scratch_shapes=[
            pltpu.VMEM((512, 768), jnp.bfloat16),
            pltpu.VMEM((NWB * 512, 128), f32),
            pltpu.VMEM((OWNERS * 16, 128), f32),
            pltpu.VMEM((OWNERS * 16 + 16, 128), f32),
            pltpu.VMEM((OWNERS * 8 + 8, 128), f32),
            pltpu.VMEM((OWNERS * 16 + 16, 128), f32),
            pltpu.VMEM((OWNERS, 128), f32),
        ]
        + flux_scratch,
        name="remap_send",
    )(tab, tab, flux_rows, above, below, before, after, diffusivity, remap_bank.reshape(NWB, 768, 128))
    arrived = lax.all_to_all(outgoing, ("gx", "gy"), split_axis=0, concat_axis=0, tiled=True)
    ocean = pl.pallas_call(
        ocean_kernel,
        out_shape=jax.ShapeDtypeStruct((F * OXD, OYD), f32),
        in_specs=[vmem] * 6,
        out_specs=vmem,
        scratch_shapes=[
            pltpu.VMEM((528, OWNERS * 16), jnp.bfloat16),
            pltpu.VMEM((48, 256), f32),
            pltpu.VMEM((40, 8, 256), f32),
            pltpu.VMEM((40, 8, 256), f32),
        ],
        name="ocean",
    )(arrived, diffusivity, above, below, before, after)
    return ocean.reshape(F, OXD, OYD)


def solution(mesh):
    in_specs = (
        P(None, "gx", "gy"),
        P("gx", "gy"),
        P(),
        P(("gx", "gy")),
        P(("gx", "gy")),
        P(("gx", "gy")),
        P(("gx", "gy")),
    )
    return jax.shard_map(local, mesh=mesh, in_specs=in_specs, out_specs=P(None, "gx", "gy"), check_vma=False)
```

time: 72.9 us -> 66.7 us (0.915)
  local copies, waits for them, and re-layouts: 4.77 us -> 0.61 us
  blocking collectives: 30.1 us -> 33.1 us
  waiting for transfers between devices: 4.92 us -> 1.97 us
  Pallas kernels: 22.7 us -> 21 us
  other arithmetic: 0.99 us -> 0 us
    pallas_call x1, Pallas kernels: 18.8 us -> 14.4 us  [local(): pl.pallas_call(send_kernel, out_shape=jax.ShapeDtypeStruct((OWNERS, 3, 16...]
    all_to_all x1, blocking collectives: 30.1 us -> 33.1 us  [local(): lax.all_to_all(outgoing, ('gx', 'gy'), split_axis=0, concat_axis=0, tiled...]
    ppermute x4, waiting for transfers between devices: 4.92 us -> 1.97 us  [shift(): return lax.ppermute(x, axis, [(i, (i + by) % count) for i in range(count)])]
    pallas_call x0 -> x1, Pallas kernels: none -> 2.76 us  [local(): pl.pallas_call(prepare_kernel, out_shape=[jax.ShapeDtypeStruct((48, 128),...]
    slice x2 -> x0, local copies, waits for them, and re-layouts: 2.04 us -> none  [the longest x1 1.16 us: gy_message(): flux[:, :, j]]
    another operation x1 -> x0, local copies, waits for them, and re-layouts: 1.83 us -> none  [record_table(): return jnp.stack(rows)]
    concatenate x2 -> x0, other arithmetic: 0.73 us -> none  [the longest x1 0.73 us: gx_message(): jnp.concatenate([flux[:, i, :128], flux[:, i, 128:], diffusivity], axis=0)]
  transfers between devices with their start and end apart: 4 -> 4, of which waited for: 1 -> 1; matrix products, arithmetic and copies ran while one was open for 5% -> 0% of each run, Pallas kernels for 0% -> 0%
where the time goes in v2:
time: 66.7 us; the launch traced here: 66.4 us
  blocking collectives  33.1 us (50%)
  Pallas kernels  21 us (31%)
  starting transfers between devices  9.56 us (14%)
  waiting for transfers between devices  1.97 us (3%)
    all_to_all x1, blocking collectives, local(): lax.all_to_all(outgoing, ('gx', 'gy'), split_axis=0, concat_axis=0, tiled...  33.1 us
    pallas_call x1, Pallas kernels, local(): pl.pallas_call(send_kernel, out_shape=jax.ShapeDtypeStruct((OWNERS, 3, 16...  14.4 us
    ppermute x4, starting transfers between devices, shift(): return lax.ppermute(x, axis, [(i, (i + by) % count) for i in range(count)])  9.56 us
    pallas_call x1, Pallas kernels, local(): pl.pallas_call(ocean_kernel, out_shape=jax.ShapeDtypeStruct((F * OXD, OYD...  3.87 us
    pallas_call x1, Pallas kernels, local(): pl.pallas_call(prepare_kernel, out_shape=[jax.ShapeDtypeStruct((48, 128),...  2.76 us
    ppermute x4, waiting for transfers between devices, shift(): return lax.ppermute(x, axis, [(i, (i + by) % count) for i in range(count)])  1.97 us
  transfers between devices with their start and end apart: 4, of which 1 were waited for; matrix products, arithmetic and copies ran while one was open for 0% of the time, Pallas kernels for 0%

profile of v2, /device:TPU:0, one launch (start us, length us, event | category | flops | bytes accessed | tf_op | source)
XLA Modules:
  0.0 66.4 jit_solution(2012388798858249593)
XLA Ops:
  0.0 2.8 %prepare.1 = (f32[48,128]{1,0:T(8,128)}, f32[48,128]{1,0:T(8,128)}, f32[40,128]{1,0:T(8,128)}, f32[40,128]{1,0:T(8,128)}, s32[24,128]{1,0:T(8,128)}) custom-call(f32[512,256]{1,0:T(8,128)} %bitcast.8, f32[32,128]{1,0:T(8,128)} %diff.5, s32[1,128]{1,0:T(1,128)} %bitcast.10, s32[1,128]{1,0:T(1,128)} %bitcast.11, s32[1,128]{1,0:T(1,128)} %bitcast.12, ...), custom_call_target="tpu_custom_call" | custom-call | tf_op jit(solution)/shard_map/prepare/pallas_call | solution.py:344
  2.8 0.0 collective-permute-start
  2.8 2.9 %collective-permute-start.1 = (f32[48,128]{1,0:T(8,128)}, f32[48,128]{1,0:T(8,128)S(1)}, u32[]{:S(2)}, u32[]{:S(2)}) collective-permute-start(f32[48,128]{1,0:T(8,128)} %get-tuple-element.12), channel_id=1, source_target_pairs={{0,112},{16,0},{32,16},{48,32},{64,48},{80,64},{96,80},{112,96},{1... | collective-permute-start | bytes 73736 | tf_op jit(solution)/shard_map/ppermute | solution.py:356
  5.7 2.0 %collective-permute-start.2 = (f32[40,128]{1,0:T(8,128)}, f32[40,128]{1,0:T(8,128)S(1)}, u32[]{:S(2)}, u32[]{:S(2)}) collective-permute-start(f32[40,128]{1,0:T(8,128)} %get-tuple-element.13), channel_id=1, source_target_pairs={{0,1},{1,2},{2,3},{3,4},{4,5},{5,6},{6,7},{7,8},{8,9},{9,10},{10,1... | collective-permute-start | bytes 61448 | tf_op jit(solution)/shard_map/ppermute | solution.py:356
  7.8 4.6 %collective-permute-start.3 = (f32[40,128]{1,0:T(8,128)}, f32[40,128]{1,0:T(8,128)S(1)}, u32[]{:S(2)}, u32[]{:S(2)}) collective-permute-start(f32[40,128]{1,0:T(8,128)} %get-tuple-element.14), channel_id=1, source_target_pairs={{0,15},{1,0},{2,1},{3,2},{4,3},{5,4},{6,5},{7,6},{8,7},{9,8},{10,9... | collective-permute-start | bytes 61448 | tf_op jit(solution)/shard_map/ppermute | solution.py:356
  12.3 2.0 %collective-permute-done.2.before = f32[40,128]{1,0:T(8,128)S(1)} collective-permute-done((f32[40,128]{1,0:T(8,128)}, f32[40,128]{1,0:T(8,128)S(1)}, u32[]{:S(2)}, u32[]{:S(2)}) %collective-permute-start.2) | collective-permute-done | bytes 20512 | tf_op jit(solution)/shard_map/ppermute | solution.py:356
  14.3 0.0 copy-start.2
  14.3 0.0 collective-permute-done.3.after
  14.3 0.0 copy-start.3
  14.3 0.0 collective-permute-done.above
  14.3 0.0 copy-start
  14.3 0.0 collective-permute-done.1.below
  14.3 0.0 copy-start.1
  14.3 0.6 copy-done.2
  14.9 0.0 copy-done.3
  14.9 0.0 copy-done
  14.9 0.0 copy-done.1
  15.0 14.4 %remap_send.1 = bf16[128,3,16,128]{3,2,1,0:T(8,128)(2,1)} custom-call(s32[24,128]{1,0:T(8,128)} %get-tuple-element.10.tab.tabv, s32[24,128]{1,0:T(8,128)} %get-tuple-element.10.tab.tabv, f32[512,256]{1,0:T(8,128)} %bitcast.9, f32[48,128]{1,0:T(8,128)} %copy-done, f32[48,128]{1,0:T(8,128)} %copy-done.1, f32[40,128]{1,0:T(8,128)} %copy-done.2, ...), custom_call_target="tpu_custom_call" | custom-call | tf_op jit(solution)/shard_map/remap_send/pallas_call | solution.py:363
  29.4 33.1 %all_to_all.5.recv = bf16[128,3,16,128]{3,2,1,0:T(8,128)(2,1)} all-to-all(bf16[128,3,16,128]{3,2,1,0:T(8,128)(2,1)} %remap_send.1), channel_id=1, replica_groups=mesh['gx'=8,'gy'=16] {'gx','gy'}, dimensions={0} | all-to-all | bytes 3145728 | tf_op jit(solution)/shard_map/all_to_all | solution.py:380
  62.5 3.9 %ocean.1 = f32[256,128]{1,0:T(8,128)} custom-call(bf16[128,3,16,128]{3,2,1,0:T(8,128)(2,1)} %all_to_all.5.recv, f32[32,128]{1,0:T(8,128)} %diff.5, f32[48,128]{1,0:T(8,128)} %copy-done, f32[48,128]{1,0:T(8,128)} %copy-done.1, f32[40,128]{1,0:T(8,128)} %copy-done.2, f32[40,128]{1,0:T(8,128)} %copy-done.3), custom_call_target="tpu_custom_call" | custom-call | tf_op jit(solution)/shard_map/ocean/pallas_call | solution.py:381
Async XLA Ops:
  2.8 11.5 %collective-permute-start = (f32[48,128]{1,0:T(8,128)}, f32[48,128]{1,0:T(8,128)S(1)}, u32[]{:S(2)}, u32[]{:S(2)}) collective-permute-start(f32[48,128]{1,0:T(8,128)} %get-tuple-element.11), channel_id=1, source_target_pairs={{0,16},{16,32},{32,48},{48,64},{64,80},{80,96},{96,112},{112,0},{1... | collective-permute-start | bytes 73736 | tf_op jit(solution)/shard_map/ppermute | solution.py:356
  2.8 11.5 %collective-permute-start.1 = (f32[48,128]{1,0:T(8,128)}, f32[48,128]{1,0:T(8,128)S(1)}, u32[]{:S(2)}, u32[]{:S(2)}) collective-permute-start(f32[48,128]{1,0:T(8,128)} %get-tuple-element.12), channel_id=1, source_target_pairs={{0,112},{16,0},{32,16},{48,32},{64,48},{80,64},{96,80},{112,96},{1... | collective-permute-start | bytes 73736 | tf_op jit(solution)/shard_map/ppermute | solution.py:356
  5.7 8.6 %collective-permute-start.2 = (f32[40,128]{1,0:T(8,128)}, f32[40,128]{1,0:T(8,128)S(1)}, u32[]{:S(2)}, u32[]{:S(2)}) collective-permute-start(f32[40,128]{1,0:T(8,128)} %get-tuple-element.13), channel_id=1, source_target_pairs={{0,1},{1,2},{2,3},{3,4},{4,5},{5,6},{6,7},{7,8},{8,9},{9,10},{10,1... | collective-permute-start | bytes 61448 | tf_op jit(solution)/shard_map/ppermute | solution.py:356
  7.8 6.5 %collective-permute-start.3 = (f32[40,128]{1,0:T(8,128)}, f32[40,128]{1,0:T(8,128)S(1)}, u32[]{:S(2)}, u32[]{:S(2)}) collective-permute-start(f32[40,128]{1,0:T(8,128)} %get-tuple-element.14), channel_id=1, source_target_pairs={{0,15},{1,0},{2,1},{3,2},{4,3},{5,4},{6,5},{7,6},{8,7},{9,8},{10,9... | collective-permute-start | bytes 61448 | tf_op jit(solution)/shard_map/ppermute | solution.py:356
  14.3 0.6 copy-start.2
  14.3 0.6 copy-start.3
  14.3 0.6 copy-start
  14.3 0.6 copy-start.1

commit v3 on v2

--- a/solution.py
+++ b/solution.py
@@ -4,6 +4,7 @@
 from jax.experimental import pallas as pl
 from jax.experimental.pallas import tpu as pltpu
 from jax.sharding import PartitionSpec as P
+
 
 F = 8
 AXD, AYD = 64, 256
@@ -24,7 +25,7 @@
 
 
 def swap_blocks(v):
-    block = lanes((8, 128)) // 16
+    block = lanes(v[0].shape) // 16
     for s in range(3):
         d = 1 << s
         high = (block & d) != 0
@@ -32,8 +33,12 @@
         for p in range(8):
             if not p & d:
                 a, b = v[p], v[p | d]
-                n[p] = jnp.where(high, pltpu.roll(b, 16 * d, 1), a)
-                n[p | d] = jnp.where(high, b, pltpu.roll(a, 128 - 16 * d, 1))
+                if d == 4:
+                    up = down = pltpu.roll(jnp.where(high, a, b), 64, 1)
+                else:
+                    up, down = pltpu.roll(b, 16 * d, 1), pltpu.roll(a, 128 - 16 * d, 1)
+                n[p] = jnp.where(high, up, a)
+                n[p | d] = jnp.where(high, b, down)
         v = n
     return v
 
@@ -47,7 +52,21 @@
     return jnp.where((gx >= 0) & (gx < NGX) & (gy >= 0) & (gy < NGY), gx * NGY + gy, OWNERS)
 
 
-def prepare_kernel(flux_in, diff, owner_in, source_in, target_in, weight_in, down, up, after, before, tab, flux, sems):
+def even(axis):
+    return lax.axis_index(axis) % 2 == 0
+
+
+def sides_of(from_c, from_x, from_a, from_b):
+    even_x, even_y = even("gx"), even("gy")
+    return (
+        lambda lo, hi: jnp.where(even_x, from_x[lo:hi, :], from_c[lo:hi, :]),
+        lambda lo, hi: jnp.where(even_x, from_c[lo:hi, :], from_x[lo:hi, :]),
+        lambda lo, hi: jnp.where(even_y, from_b[lo:hi, :], from_a[lo:hi, :]),
+        lambda lo, hi: jnp.where(even_y, from_a[lo:hi, :], from_b[lo:hi, :]),
+    )
+
+
+def prepare_kernel(flux_in, diff, owner_in, source_in, target_in, weight_in, to_c, to_x, to_a, to_b, tab, flux, sems):
     copies = load_flux(flux_in, flux, sems)
     for copy in copies:
         copy.start()
@@ -82,9 +101,9 @@
     for n in range(len(rows), TAB_ROWS):
         tab[n : n + 1, :] = slot
 
-    for to in (down, up):
+    for to in (to_c, to_x):
         to[16:48, :] = diff[...]
-    for to in (after, before):
+    for to in (to_a, to_b):
         to[8:40, :] = diff[...]
     for copy in copies:
         copy.wait()
@@ -92,19 +111,21 @@
     def row(i, g):
         return flux[g, pl.ds(i, 8, stride=AXD), :]
 
+    even_x, even_y = even("gx"), even("gy")
     for g in range(2):
-        down[g * 8 : g * 8 + 8, :] = row(AXD - 1, g)
-        up[g * 8 : g * 8 + 8, :] = row(0, g)
+        bottom, top = row(AXD - 1, g), row(0, g)
+        to_c[g * 8 : g * 8 + 8, :] = jnp.where(even_x, bottom, top)
+        to_x[g * 8 : g * 8 + 8, :] = jnp.where(even_x, top, bottom)
     last = jnp.zeros((8, 128), jnp.float32)
     first = jnp.zeros((8, 128), jnp.float32)
     for i in range(AXD):
         last = jnp.where(lane == i, row(i, 1)[:, 127:128], last)
         first = jnp.where(lane == i, row(i, 0)[:, 0:1], first)
-    after[0:8, :] = last
-    before[0:8, :] = first
-
-
-def send_kernel(tab, tabv, flux_in, above, below, before, after, diff, bank, out, lhs, prod, owns, pairs, sides, corners, lab, flux, sems):
+    to_a[0:8, :] = jnp.where(even_y, last, first)
+    to_b[0:8, :] = jnp.where(even_y, first, last)
+
+
+def send_kernel(tab, tabv, flux_in, from_c, from_x, from_a, from_b, diff, bank, out, lhs, prod, owns, pairs, sides, corners, lab, flux, sems):
     copies = load_flux(flux_in, flux, sems)
     for copy in copies:
         copy.start()
@@ -141,13 +162,16 @@
     lax.fori_loop(0, OWNERS, clear, 0, unroll=4)
 
     wide = lanes((8, 256))
-    left, right = before[0:8, :], after[0:8, :]
+    above, below, before, after = sides_of(from_c, from_x, from_a, from_b)
+    left, right = before(0, 8), after(0, 8)
+    top = jnp.concatenate([above(0, 8), above(8, 16)], axis=1)
+    bottom = jnp.concatenate([below(0, 8), below(8, 16)], axis=1)
 
     def row(i):
         if i < 0:
-            return jnp.concatenate([above[0:8, :], above[8:16, :]], axis=1)
+            return top
         if i >= AXD:
-            return jnp.concatenate([below[0:8, :], below[8:16, :]], axis=1)
+            return bottom
         return jnp.concatenate([flux[g, pl.ds(i, 8, stride=AXD), :] for g in range(2)], axis=1)
 
     for copy in copies:
@@ -167,11 +191,12 @@
                     prv = jnp.where(wide == 0, left[:, i : i + 1], pltpu.roll(x[a + 1], 1, 1))
                     vals.append((nxt - prv) * 0.5)
             for h in range(2):
-                y = [swap_blocks([vals[h * 8 + q][:, g * 128 : (g + 1) * 128] for q in range(8)]) for g in range(2)]
-                for q in range(8):
-                    lhs[pl.ds((ti * 8 + q) * 16, 16), pl.ds(k * 256 + h * 128, 128)] = jnp.concatenate(
-                        [y[0][q], y[1][q]], axis=0
-                    ).astype(jnp.bfloat16)
+                packed = [
+                    jnp.concatenate([vals[h * 8 + q][:, :128], vals[h * 8 + q][:, 128:]], axis=0).astype(jnp.bfloat16)
+                    for q in range(8)
+                ]
+                for q, tile in enumerate(swap_blocks(packed)):
+                    lhs[pl.ds((ti * 8 + q) * 16, 16), pl.ds(k * 256 + h * 128, 128)] = tile
 
     def product(n, carry):
         rhs = jnp.concatenate([bank[2 * n], bank[2 * n + 1]], axis=1)
@@ -223,9 +248,9 @@
     lax.fori_loop(0, OWNERS, convert, 0, unroll=8)
 
 
-def ocean_kernel(recv, diff, above, below, before, after, out, onehot, dext, u0, u1):
+def ocean_kernel(recv, diff, from_c, from_x, from_a, from_b, out, onehot, dext, u0, u1):
     lane = lanes((8, 128))
-    a_of, b_of = lane // 16, lane % 16
+    b_of = lane % 16
     K = OWNERS * 16
     own_in = recv[:, 0].reshape(K, 128)
     pair_in = recv[:, 1].reshape(K, 128)
@@ -295,6 +320,8 @@
         u0[a - 4, :, 0:128] = rows[a]
     put_side(tile(sides, 16), [(a, 36 + a) for a in range(4)] + [(a, a - 4) for a in range(4, 8)])
 
+    above, below, before, after = sides_of(from_c, from_x, from_a, from_b)
+
     def flag(du, dv):
         return jnp.where(neighbour(du, dv) < OWNERS, 1.0, 0.0)
 
@@ -309,14 +336,14 @@
     def ends(left, right):
         return jnp.where(lane < 4, right, jnp.where(lane >= 124, left, 0.0))
 
-    dext[0:8, 0:128] = above[40:48, :] * flag(-1, 0)
-    dext[40:48, 0:128] = below[16:24, :] * flag(1, 0)
+    dext[0:8, 0:128] = above(40, 48) * flag(-1, 0)
+    dext[40:48, 0:128] = below(16, 24) * flag(1, 0)
     dext[8:40, 0:128] = diff[...]
     dext[0:8, 128:256] = ends(corner(-1, -1), corner(-1, 1))
     dext[40:48, 128:256] = ends(corner(1, -1), corner(1, 1))
     for q in range(4):
         dext[8 + q * 8 : 16 + q * 8, 128:256] = ends(
-            before[8 + q * 8 : 16 + q * 8, :] * flag(0, -1), after[8 + q * 8 : 16 + q * 8, :] * flag(0, 1)
+            before(8 + q * 8, 16 + q * 8) * flag(0, -1), after(8 + q * 8, 16 + q * 8) * flag(0, 1)
         )
 
     src, dst = u0, u1
@@ -341,7 +368,7 @@
     flux_scratch = [pltpu.VMEM((2, F * AXD, 128), jnp.float32), pltpu.SemaphoreType.DMA((2,))]
     records = [x.reshape(1, RECS) for x in (rec_owner, rec_source, rec_target, rec_weight)]
     f32, i32 = jnp.float32, jnp.int32
-    down, up, right, left, tab = pl.pallas_call(
+    to_c, to_x, to_a, to_b, tab = pl.pallas_call(
         prepare_kernel,
         out_shape=[jax.ShapeDtypeStruct((48, 128), f32)] * 2
         + [jax.ShapeDtypeStruct((40, 128), f32)] * 2
@@ -352,13 +379,12 @@
         name="prepare",
     )(flux_rows, diffusivity, *records)
 
-    def shift(x, axis, count, by):
-        return lax.ppermute(x, axis, [(i, (i + by) % count) for i in range(count)])
-
-    above = shift(down, "gx", NGX, 1)
-    below = shift(up, "gx", NGX, -1)
-    before = shift(right, "gy", NGY, 1)
-    after = shift(left, "gy", NGY, -1)
+    def swap(x, axis, count, odd):
+        return lax.ppermute(x, axis, [(i, (((i + odd) ^ 1) - odd) % count) for i in range(count)])
+
+    came = []
+    for x, axis, count, odd in ((to_c, "gx", NGX, 0), (to_x, "gx", NGX, 1), (to_a, "gy", NGY, 0), (to_b, "gy", NGY, 1)):
+        came.append(swap(x, axis, count, odd))
 
     outgoing = pl.pallas_call(
         send_kernel,
@@ -376,7 +402,7 @@
         ]
         + flux_scratch,
         name="remap_send",
-    )(tab, tab, flux_rows, above, below, before, after, diffusivity, remap_bank.reshape(NWB, 768, 128))
+    )(tab, tab, flux_rows, *came, diffusivity, remap_bank.reshape(NWB, 768, 128))
     arrived = lax.all_to_all(outgoing, ("gx", "gy"), split_axis=0, concat_axis=0, tiled=True)
     ocean = pl.pallas_call(
         ocean_kernel,
@@ -390,7 +416,7 @@
             pltpu.VMEM((40, 8, 256), f32),
         ],
         name="ocean",
-    )(arrived, diffusivity, above, below, before, after)
+    )(arrived, diffusivity, *came)
     return ocean.reshape(F, OXD, OYD)
 
 

time: 66.7 us -> 63.5 us (0.952)
  Pallas kernels: 21 us -> 18.4 us
  blocking collectives: 33.1 us -> 31.8 us
    pallas_call x1, Pallas kernels: 14.4 us -> 11.7 us  [local(): pl.pallas_call(send_kernel, out_shape=jax.ShapeDtypeStruct((OWNERS, 3, 16...]
    all_to_all x1, blocking collectives: 33.1 us -> 31.8 us  [local(): lax.all_to_all(outgoing, ('gx', 'gy'), split_axis=0, concat_axis=0, tiled...]
where the time goes in v3:
time: 63.5 us; the launch traced here: 63.1 us
  blocking collectives  31.8 us (50%)
  Pallas kernels  18.4 us (29%)
  starting transfers between devices  9.95 us (16%)
  waiting for transfers between devices  2.34 us (4%)
    all_to_all x1, blocking collectives, local(): lax.all_to_all(outgoing, ('gx', 'gy'), split_axis=0, concat_axis=0, tiled...  31.8 us
    pallas_call x1, Pallas kernels, local(): pl.pallas_call(send_kernel, out_shape=jax.ShapeDtypeStruct((OWNERS, 3, 16...  11.7 us
    ppermute x4, starting transfers between devices, swap(): lax.ppermute(x, axis, [(i, ((i + odd ^ 1) - odd) % count) for i in range(...  9.95 us
    pallas_call x1, Pallas kernels, local(): pl.pallas_call(ocean_kernel, out_shape=jax.ShapeDtypeStruct((F * OXD, OYD...  3.88 us
    pallas_call x1, Pallas kernels, local(): pl.pallas_call(prepare_kernel, out_shape=[jax.ShapeDtypeStruct((48, 128),...  2.77 us
    ppermute x4, waiting for transfers between devices, swap(): lax.ppermute(x, axis, [(i, ((i + odd ^ 1) - odd) % count) for i in range(...  2.34 us
  transfers between devices with their start and end apart: 4, of which 1 were waited for; matrix products, arithmetic and copies ran while one was open for 0% of the time, Pallas kernels for 0%

profile of v3, /device:TPU:0, one launch (start us, length us, event | category | flops | bytes accessed | tf_op | source)
XLA Modules:
  0.0 63.1 jit_solution(6891644982227269956)
XLA Ops:
  0.0 2.8 %prepare.1 = (f32[48,128]{1,0:T(8,128)}, f32[48,128]{1,0:T(8,128)}, f32[40,128]{1,0:T(8,128)}, f32[40,128]{1,0:T(8,128)}, s32[24,128]{1,0:T(8,128)}) custom-call(f32[512,256]{1,0:T(8,128)} %bitcast.8, f32[32,128]{1,0:T(8,128)} %diff.5, s32[1,128]{1,0:T(1,128)} %bitcast.10, s32[1,128]{1,0:T(1,128)} %bitcast.11, s32[1,128]{1,0:T(1,128)} %bitcast.12, ...), custom_call_target="tpu_custom_call" | custom-call | tf_op jit(solution)/shard_map/prepare/pallas_call | solution.py:371
  2.8 0.1 collective-permute-start
  2.9 3.0 %collective-permute-start.1 = (f32[48,128]{1,0:T(8,128)}, f32[48,128]{1,0:T(8,128)S(1)}, u32[]{:S(2)}, u32[]{:S(2)}) collective-permute-start(f32[48,128]{1,0:T(8,128)} %get-tuple-element.12), channel_id=1, source_target_pairs={{0,112},{16,32},{32,16},{48,64},{64,48},{80,96},{96,80},{112,0},{1... | collective-permute-start | bytes 73736 | tf_op jit(solution)/shard_map/ppermute | solution.py:383
  5.8 1.9 %collective-permute-start.2 = (f32[40,128]{1,0:T(8,128)}, f32[40,128]{1,0:T(8,128)S(1)}, u32[]{:S(2)}, u32[]{:S(2)}) collective-permute-start(f32[40,128]{1,0:T(8,128)} %get-tuple-element.13), channel_id=1, source_target_pairs={{0,1},{1,0},{2,3},{3,2},{4,5},{5,4},{6,7},{7,6},{8,9},{9,8},{10,11... | collective-permute-start | bytes 61448 | tf_op jit(solution)/shard_map/ppermute | solution.py:383
  7.8 5.0 %collective-permute-start.3 = (f32[40,128]{1,0:T(8,128)}, f32[40,128]{1,0:T(8,128)S(1)}, u32[]{:S(2)}, u32[]{:S(2)}) collective-permute-start(f32[40,128]{1,0:T(8,128)} %get-tuple-element.14), channel_id=1, source_target_pairs={{0,15},{1,2},{2,1},{3,4},{4,3},{5,6},{6,5},{7,8},{8,7},{9,10},{10,... | collective-permute-start | bytes 61448 | tf_op jit(solution)/shard_map/ppermute | solution.py:383
  12.7 0.0 collective-permute-done.2.from_a
  12.7 0.0 copy-start.2
  12.7 2.3 %collective-permute-done.3.from_b = f32[40,128]{1,0:T(8,128)S(1)} collective-permute-done((f32[40,128]{1,0:T(8,128)}, f32[40,128]{1,0:T(8,128)S(1)}, u32[]{:S(2)}, u32[]{:S(2)}) %collective-permute-start.3) | collective-permute-done | bytes 20512 | tf_op jit(solution)/shard_map/ppermute | solution.py:383
  15.1 0.0 copy-start.3
  15.1 0.0 collective-permute-done.from_c
  15.1 0.0 copy-start
  15.1 0.0 collective-permute-done.1.from_x
  15.1 0.0 copy-start.1
  15.1 0.0 copy-done.2
  15.1 0.6 copy-done.3
  15.7 0.0 copy-done
  15.7 0.0 copy-done.1
  15.7 11.7 %remap_send.1 = bf16[128,3,16,128]{3,2,1,0:T(8,128)(2,1)} custom-call(s32[24,128]{1,0:T(8,128)} %get-tuple-element.10.tab.tabv, s32[24,128]{1,0:T(8,128)} %get-tuple-element.10.tab.tabv, f32[512,256]{1,0:T(8,128)} %bitcast.9, f32[48,128]{1,0:T(8,128)} %copy-done, f32[48,128]{1,0:T(8,128)} %copy-done.1, f32[40,128]{1,0:T(8,128)} %copy-done.2, ...), custom_call_target="tpu_custom_call" | custom-call | tf_op jit(solution)/shard_map/remap_send/pallas_call | solution.py:389
  27.5 31.8 %all_to_all.5.recv = bf16[128,3,16,128]{3,2,1,0:T(8,128)(2,1)} all-to-all(bf16[128,3,16,128]{3,2,1,0:T(8,128)(2,1)} %remap_send.1), channel_id=1, replica_groups=mesh['gx'=8,'gy'=16] {'gx','gy'}, dimensions={0} | all-to-all | bytes 3145728 | tf_op jit(solution)/shard_map/all_to_all | solution.py:406
  59.3 3.9 %ocean.1 = f32[256,128]{1,0:T(8,128)} custom-call(bf16[128,3,16,128]{3,2,1,0:T(8,128)(2,1)} %all_to_all.5.recv, f32[32,128]{1,0:T(8,128)} %diff.5, f32[48,128]{1,0:T(8,128)} %copy-done, f32[48,128]{1,0:T(8,128)} %copy-done.1, f32[40,128]{1,0:T(8,128)} %copy-done.2, f32[40,128]{1,0:T(8,128)} %copy-done.3), custom_call_target="tpu_custom_call" | custom-call | tf_op jit(solution)/shard_map/ocean/pallas_call | solution.py:407
Async XLA Ops:
  2.8 12.3 %collective-permute-start = (f32[48,128]{1,0:T(8,128)}, f32[48,128]{1,0:T(8,128)S(1)}, u32[]{:S(2)}, u32[]{:S(2)}) collective-permute-start(f32[48,128]{1,0:T(8,128)} %get-tuple-element.11), channel_id=1, source_target_pairs={{0,16},{16,0},{32,48},{48,32},{64,80},{80,64},{96,112},{112,96},{1... | collective-permute-start | bytes 73736 | tf_op jit(solution)/shard_map/ppermute | solution.py:383
  2.9 12.2 %collective-permute-start.1 = (f32[48,128]{1,0:T(8,128)}, f32[48,128]{1,0:T(8,128)S(1)}, u32[]{:S(2)}, u32[]{:S(2)}) collective-permute-start(f32[48,128]{1,0:T(8,128)} %get-tuple-element.12), channel_id=1, source_target_pairs={{0,112},{16,32},{32,16},{48,64},{64,48},{80,96},{96,80},{112,0},{1... | collective-permute-start | bytes 73736 | tf_op jit(solution)/shard_map/ppermute | solution.py:383
  5.8 6.9 %collective-permute-start.2 = (f32[40,128]{1,0:T(8,128)}, f32[40,128]{1,0:T(8,128)S(1)}, u32[]{:S(2)}, u32[]{:S(2)}) collective-permute-start(f32[40,128]{1,0:T(8,128)} %get-tuple-element.13), channel_id=1, source_target_pairs={{0,1},{1,0},{2,3},{3,2},{4,5},{5,4},{6,7},{7,6},{8,9},{9,8},{10,11... | collective-permute-start | bytes 61448 | tf_op jit(solution)/shard_map/ppermute | solution.py:383
  7.8 7.3 %collective-permute-start.3 = (f32[40,128]{1,0:T(8,128)}, f32[40,128]{1,0:T(8,128)S(1)}, u32[]{:S(2)}, u32[]{:S(2)}) collective-permute-start(f32[40,128]{1,0:T(8,128)} %get-tuple-element.14), channel_id=1, source_target_pairs={{0,15},{1,2},{2,1},{3,4},{4,3},{5,6},{6,5},{7,8},{8,7},{9,10},{10,... | collective-permute-start | bytes 61448 | tf_op jit(solution)/shard_map/ppermute | solution.py:383
  12.7 2.4 %copy-start.2 = (f32[40,128]{1,0:T(8,128)}, f32[40,128]{1,0:T(8,128)S(1)}, u32[]{:S(2)}) copy-start(f32[40,128]{1,0:T(8,128)S(1)} %collective-permute-done.2.from_a) | copy-start | bytes 61444
  15.1 0.6 copy-start.3
  15.1 0.6 copy-start
  15.1 0.6 copy-start.1

commit v4 on v3

--- a/solution.py
+++ b/solution.py
@@ -43,10 +43,6 @@
     return v
 
 
-def load_flux(flux_in, flux, sems):
-    return [pltpu.make_async_copy(flux_in.at[:, pl.ds(g * 128, 128)], flux.at[g], sems.at[g]) for g in range(2)]
-
-
 def neighbour(du, dv):
     gx, gy = lax.axis_index("gx") + du, lax.axis_index("gy") + dv
     return jnp.where((gx >= 0) & (gx < NGX) & (gy >= 0) & (gy < NGY), gx * NGY + gy, OWNERS)
@@ -66,12 +62,13 @@
     )
 
 
-def prepare_kernel(flux_in, diff, owner_in, source_in, target_in, weight_in, to_c, to_x, to_a, to_b, tab, flux, sems):
-    copies = load_flux(flux_in, flux, sems)
+def prepare_kernel(flux_in, diff_in, ids, to_c, to_x, to_a, to_b, tab, flux, diff, sems):
+    moves = [(diff_in, diff)] + [(flux_in.at[:, pl.ds(g * 128, 128)], flux.at[g]) for g in range(2)]
+    copies = [pltpu.make_async_copy(src, dst, sems.at[n]) for n, (src, dst) in enumerate(moves)]
     for copy in copies:
         copy.start()
     lane = lanes((8, 128))
-    owner, source, target, weight = owner_in[...], source_in[...], target_in[...], weight_in[...]
+    owner, source, target, weight = (ids[n : n + 1, :] for n in range(4))
     across = jnp.broadcast_to(owner, (RECS, RECS))
     along = jnp.transpose(across.astype(jnp.float32)).astype(jnp.int32)
     sub = lax.broadcasted_iota(jnp.int32, (RECS, RECS), 0)
@@ -101,11 +98,12 @@
     for n in range(len(rows), TAB_ROWS):
         tab[n : n + 1, :] = slot
 
+    copies[0].wait()
     for to in (to_c, to_x):
         to[16:48, :] = diff[...]
     for to in (to_a, to_b):
         to[8:40, :] = diff[...]
-    for copy in copies:
+    for copy in copies[1:]:
         copy.wait()
 
     def row(i, g):
@@ -125,22 +123,59 @@
     to_b[0:8, :] = jnp.where(even_y, first, last)
 
 
-def send_kernel(tab, tabv, flux_in, from_c, from_x, from_a, from_b, diff, bank, out, lhs, prod, owns, pairs, sides, corners, lab, flux, sems):
-    copies = load_flux(flux_in, flux, sems)
+def tiles_kernel(flux, tabv, bank_in, lhs, lab, bank, sem):
+    weights = pltpu.make_async_copy(bank_in, bank, sem)
+    weights.start()
+    rows3 = lax.broadcasted_iota(jnp.int32, (128, 3 * RECS), 0)
+
+    def three(*at):
+        return jnp.concatenate([jnp.broadcast_to(tabv[n : n + 1, :], (128, RECS)) for n in at], axis=1)
+
+    going = jnp.where(three(OWNER, XTO, YTO) == rows3, 1.0, 0.0).astype(jnp.bfloat16)
+    label = jnp.where(three(PO, PX, PY) == rows3, three(VO, VX, VY), 0).astype(jnp.float32).astype(jnp.bfloat16)
+    lab[...] = lax.dot_general(going, label, (((1,), (1,)), ((), ())), preferred_element_type=jnp.float32)
+
+    wide = lanes((8, 256))
+    outside = jnp.zeros((8, 256), jnp.float32)
+
+    def row(i):
+        if i < 0 or i >= AXD:
+            return outside
+        return jnp.concatenate([flux[g, pl.ds(i, 8, stride=AXD), :] for g in range(2)], axis=1)
+
+    for ti in range(4):
+        x = [row(i) for i in range(ti * 16 - 1, ti * 16 + 17)]
+        for k in range(3):
+            vals = []
+            for a in range(16):
+                if k == 0:
+                    vals.append(x[a + 1])
+                elif k == 1:
+                    vals.append((x[a + 2] - x[a]) * 0.5)
+                else:
+                    nxt = jnp.where(wide == 255, 0.0, pltpu.roll(x[a + 1], 255, 1))
+                    prv = jnp.where(wide == 0, 0.0, pltpu.roll(x[a + 1], 1, 1))
+                    vals.append((nxt - prv) * 0.5)
+            for h in range(2):
+                packed = [
+                    jnp.concatenate([vals[h * 8 + q][:, :128], vals[h * 8 + q][:, 128:]], axis=0).astype(jnp.bfloat16)
+                    for q in range(8)
+                ]
+                for q, tile in enumerate(swap_blocks(packed)):
+                    lhs[pl.ds((ti * 8 + q) * 16, 16), pl.ds(k * 256 + h * 128, 128)] = tile
+    weights.wait()
+
+
+def send_kernel(
+    tab_in, lhs_in, lab, from_c, from_x, from_a, from_b, diff, bank, out,
+    tab, lhs, prod, owns, pairs, sides, corners, sems,
+):
+    copies = [pltpu.make_async_copy(src, dst, sems.at[n]) for n, (src, dst) in enumerate(((tab_in, tab), (lhs_in, lhs)))]
     for copy in copies:
         copy.start()
     lane = lanes((8, 128))
     sub = lax.broadcasted_iota(jnp.int32, (8, 128), 0)
     a_of, b_of = lane // 16, lane % 16
-
-    rows3 = lax.broadcasted_iota(jnp.int32, (128, 3 * RECS), 0)
-
-    def three(*at):
-        return jnp.concatenate([jnp.broadcast_to(tabv[n : n + 1, :], (128, RECS)) for n in at], axis=1)
-
-    going = jnp.where(three(OWNER, XTO, YTO) == rows3, 1.0, 0.0).astype(jnp.bfloat16)
-    label = jnp.where(three(PO, PX, PY) == rows3, three(VO, VX, VY), 0).astype(jnp.float32).astype(jnp.bfloat16)
-    lab[...] = lax.dot_general(going, label, (((1,), (1,)), ((), ())), preferred_element_type=jnp.float32)
     is_label = (a_of == 2) & (b_of >= 4) & (b_of < 12) | (a_of == 3) & (b_of >= 4) & (b_of < 6)
     absent = jnp.where(is_label, ABSENT, 0.0)
     offset = (sub - 1).astype(jnp.float32)
@@ -160,43 +195,34 @@
         return carry
 
     lax.fori_loop(0, OWNERS, clear, 0, unroll=4)
-
-    wide = lanes((8, 256))
-    above, below, before, after = sides_of(from_c, from_x, from_a, from_b)
-    left, right = before(0, 8), after(0, 8)
-    top = jnp.concatenate([above(0, 8), above(8, 16)], axis=1)
-    bottom = jnp.concatenate([below(0, 8), below(8, 16)], axis=1)
-
-    def row(i):
-        if i < 0:
-            return top
-        if i >= AXD:
-            return bottom
-        return jnp.concatenate([flux[g, pl.ds(i, 8, stride=AXD), :] for g in range(2)], axis=1)
-
     for copy in copies:
         copy.wait()
+
+    above, below, before, after = sides_of(from_c, from_x, from_a, from_b)
+    lane16 = lanes((16, 128))
+
+    def add(ti, q, k, h, lo, hi, what):
+        rows_at, cols_at = pl.ds((ti * 8 + q) * 16, 16), pl.ds(k * 256 + h * 128, 128)
+        if hi - lo == 8:
+            none = jnp.zeros((8, 128), jnp.float32)
+            what = jnp.concatenate([what, none] if lo == 0 else [none, what], axis=0)
+        lhs[rows_at, cols_at] = (lhs[rows_at, cols_at].astype(jnp.float32) + what).astype(jnp.bfloat16)
+
+    top, bottom = above(0, 16) * -0.5, below(0, 16) * 0.5
+    for q in range(8):
+        add(0, q, 1, 0, 0, 16, jnp.where(lane16 < 16, pltpu.roll(top, (128 - 16 * q) % 128, 1), 0.0))
+        add(3, q, 1, 1, 0, 16, jnp.where(lane16 >= 112, pltpu.roll(bottom, 112 - 16 * q, 1), 0.0))
+    left, right = before(0, 8) * -0.5, after(0, 8) * 0.5
     for ti in range(4):
-        x = [row(i) for i in range(ti * 16 - 1, ti * 16 + 17)]
-        for k in range(3):
-            vals = []
-            for a in range(16):
-                i = ti * 16 + a
-                if k == 0:
-                    vals.append(x[a + 1])
-                elif k == 1:
-                    vals.append((x[a + 2] - x[a]) * 0.5)
-                else:
-                    nxt = jnp.where(wide == 255, right[:, i : i + 1], pltpu.roll(x[a + 1], 255, 1))
-                    prv = jnp.where(wide == 0, left[:, i : i + 1], pltpu.roll(x[a + 1], 1, 1))
-                    vals.append((nxt - prv) * 0.5)
-            for h in range(2):
-                packed = [
-                    jnp.concatenate([vals[h * 8 + q][:, :128], vals[h * 8 + q][:, 128:]], axis=0).astype(jnp.bfloat16)
-                    for q in range(8)
-                ]
-                for q, tile in enumerate(swap_blocks(packed)):
-                    lhs[pl.ds((ti * 8 + q) * 16, 16), pl.ds(k * 256 + h * 128, 128)] = tile
+        for h in range(2):
+            low = jnp.zeros((8, 128), jnp.float32)
+            high = jnp.zeros((8, 128), jnp.float32)
+            for q in range(8):
+                i = ti * 16 + h * 8 + q
+                low = jnp.where(lane == q * 16, left[:, i : i + 1], low)
+                high = jnp.where(lane == q * 16 + 15, right[:, i : i + 1], high)
+            add(ti, 0, 2, h, 0, 8, low)
+            add(ti, 7, 2, h, 8, 16, high)
 
     def product(n, carry):
         rhs = jnp.concatenate([bank[2 * n], bank[2 * n + 1]], axis=1)
@@ -365,19 +391,21 @@
     smem = pl.BlockSpec(memory_space=pltpu.SMEM)
     anywhere = pl.BlockSpec(memory_space=pl.ANY)
     flux_rows = flux.reshape(F * AXD, AYD)
-    flux_scratch = [pltpu.VMEM((2, F * AXD, 128), jnp.float32), pltpu.SemaphoreType.DMA((2,))]
-    records = [x.reshape(1, RECS) for x in (rec_owner, rec_source, rec_target, rec_weight)]
+    hbm = pl.BlockSpec(memory_space=pltpu.HBM)
+    records = jnp.stack([rec_owner, rec_source, rec_target, rec_weight])
     f32, i32 = jnp.float32, jnp.int32
-    to_c, to_x, to_a, to_b, tab = pl.pallas_call(
+    to_c, to_x, to_a, to_b, tab, flux_halves, diff = pl.pallas_call(
         prepare_kernel,
         out_shape=[jax.ShapeDtypeStruct((48, 128), f32)] * 2
         + [jax.ShapeDtypeStruct((40, 128), f32)] * 2
-        + [jax.ShapeDtypeStruct((TAB_ROWS, RECS), i32)],
-        in_specs=[anywhere] + [vmem] * 5,
-        out_specs=[vmem] * 5,
-        scratch_shapes=flux_scratch,
+        + [jax.ShapeDtypeStruct((TAB_ROWS, RECS), i32), jax.ShapeDtypeStruct((2, F * AXD, 128), f32)]
+        + [jax.ShapeDtypeStruct((OXD, OYD), f32)],
+        in_specs=[hbm] * 2 + [vmem],
+        out_specs=[vmem] * 7,
+        scratch_shapes=[pltpu.SemaphoreType.DMA((3,))],
         name="prepare",
-    )(flux_rows, diffusivity, *records)
+        compiler_params=pltpu.CompilerParams(vmem_limit_bytes=6 << 20),
+    )(flux_rows, diffusivity, records)
 
     def swap(x, axis, count, odd):
         return lax.ppermute(x, axis, [(i, (((i + odd) ^ 1) - odd) % count) for i in range(count)])
@@ -386,23 +414,36 @@
     for x, axis, count, odd in ((to_c, "gx", NGX, 0), (to_x, "gx", NGX, 1), (to_a, "gy", NGY, 0), (to_b, "gy", NGY, 1)):
         came.append(swap(x, axis, count, odd))
 
+    bf16 = jnp.bfloat16
+    lhs, lab, bank = pl.pallas_call(
+        tiles_kernel,
+        out_shape=[jax.ShapeDtypeStruct((512, 768), bf16), jax.ShapeDtypeStruct((OWNERS, 128), f32)]
+        + [jax.ShapeDtypeStruct((NWB, 768, 128), bf16)],
+        in_specs=[vmem, vmem, hbm],
+        out_specs=[vmem] * 3,
+        scratch_shapes=[pltpu.SemaphoreType.DMA],
+        name="tiles",
+    compiler_params=pltpu.CompilerParams(vmem_limit_bytes=8 << 20),
+    )(flux_halves, tab, remap_bank.reshape(NWB, 768, 128))
+
     outgoing = pl.pallas_call(
         send_kernel,
-        out_shape=jax.ShapeDtypeStruct((OWNERS, 3, 16, 128), jnp.bfloat16),
-        in_specs=[smem, vmem, anywhere] + [vmem] * 6,
+        out_shape=jax.ShapeDtypeStruct((OWNERS, 3, 16, 128), bf16),
+        in_specs=[anywhere] * 2 + [vmem] * 7,
         out_specs=vmem,
         scratch_shapes=[
-            pltpu.VMEM((512, 768), jnp.bfloat16),
+            pltpu.SMEM((TAB_ROWS, RECS), i32),
+            pltpu.VMEM((512, 768), bf16),
             pltpu.VMEM((NWB * 512, 128), f32),
             pltpu.VMEM((OWNERS * 16, 128), f32),
             pltpu.VMEM((OWNERS * 16 + 16, 128), f32),
             pltpu.VMEM((OWNERS * 8 + 8, 128), f32),
             pltpu.VMEM((OWNERS * 16 + 16, 128), f32),
-            pltpu.VMEM((OWNERS, 128), f32),
-        ]
-        + flux_scratch,
+            pltpu.SemaphoreType.DMA((2,)),
+        ],
         name="remap_send",
-    )(tab, tab, flux_rows, *came, diffusivity, remap_bank.reshape(NWB, 768, 128))
+        compiler_params=pltpu.CompilerParams(vmem_limit_bytes=24 << 20),
+    )(tab, lhs, lab, *came, diff, bank)
     arrived = lax.all_to_all(outgoing, ("gx", "gy"), split_axis=0, concat_axis=0, tiled=True)
     ocean = pl.pallas_call(
         ocean_kernel,
@@ -416,7 +457,8 @@
             pltpu.VMEM((40, 8, 256), f32),
         ],
         name="ocean",
-    )(arrived, diffusivity, *came)
+        compiler_params=pltpu.CompilerParams(vmem_limit_bytes=16 << 20),
+    )(arrived, diff, *came)
     return ocean.reshape(F, OXD, OYD)
 
 

time: 63.5 us -> 54.4 us (0.86)
  Pallas kernels: 18.4 us -> 11.2 us
  blocking collectives: 31.8 us -> 28.5 us
  local copies, waits for them, and re-layouts: 0.61 us -> 3.65 us
  waiting for transfers between devices: 2.34 us -> 0.01 us
  other arithmetic: 0 us -> 0.71 us
    pallas_call x1, Pallas kernels: 11.7 us -> 4.96 us  [local(): pl.pallas_call(send_kernel, out_shape=jax.ShapeDtypeStruct((OWNERS, 3, 16...]
    all_to_all x1, blocking collectives: 31.8 us -> 28.5 us  [local(): lax.all_to_all(outgoing, ('gx', 'gy'), split_axis=0, concat_axis=0, tiled...]
    pallas_call x0 -> x1, Pallas kernels: none -> 3.26 us  [local(): pl.pallas_call(tiles_kernel, out_shape=[jax.ShapeDtypeStruct((512, 768),...]
    unnamed x8 -> x6, local copies, waits for them, and re-layouts: 0.61 us -> 3.65 us
    ppermute x4, waiting for transfers between devices: 2.34 us -> 0.01 us  [swap(): lax.ppermute(x, axis, [(i, ((i + odd ^ 1) - odd) % count) for i in range(...]
    pallas_call x1, Pallas kernels: 2.77 us -> 0.55 us  [local(): pl.pallas_call(prepare_kernel, out_shape=[jax.ShapeDtypeStruct((48, 128),...]
    pallas_call x1, Pallas kernels: 3.88 us -> 2.44 us  [local(): pl.pallas_call(ocean_kernel, out_shape=jax.ShapeDtypeStruct((F * OXD, OYD...]
    another operation x0 -> x1, other arithmetic: none -> 0.71 us  [local(): records = jnp.stack([rec_owner, rec_source, rec_target, rec_weight])]
  transfers between devices with their start and end apart: 4 -> 4, of which waited for: 1 -> 0; matrix products, arithmetic and copies ran while one was open for 0% -> 0% of each run, Pallas kernels for 0% -> 6%
where the time goes in v4:
time: 54.4 us; the launch traced here: 54.1 us
  blocking collectives  28.5 us (52%)
  Pallas kernels  11.2 us (21%)
  starting transfers between devices  9.95 us (18%)
  local copies, waits for them, and re-layouts  3.65 us (7%)
  other arithmetic  0.71 us (1%)
    all_to_all x1, blocking collectives, local(): lax.all_to_all(outgoing, ('gx', 'gy'), split_axis=0, concat_axis=0, tiled...  28.5 us
    ppermute x4, starting transfers between devices, swap(): lax.ppermute(x, axis, [(i, ((i + odd ^ 1) - odd) % count) for i in range(...  9.95 us
    pallas_call x1, Pallas kernels, local(): pl.pallas_call(send_kernel, out_shape=jax.ShapeDtypeStruct((OWNERS, 3, 16...  4.96 us
    unnamed x6, local copies, waits for them, and re-layouts  3.65 us
    pallas_call x1, Pallas kernels, local(): pl.pallas_call(tiles_kernel, out_shape=[jax.ShapeDtypeStruct((512, 768),...  3.26 us
    pallas_call x1, Pallas kernels, local(): pl.pallas_call(ocean_kernel, out_shape=jax.ShapeDtypeStruct((F * OXD, OYD...  2.44 us
  transfers between devices with their start and end apart: 4, of which 0 were waited for; matrix products, arithmetic and copies ran while one was open for 0% of the time, Pallas kernels for 6%

profile of v4, /device:TPU:0, one launch (start us, length us, event | category | flops | bytes accessed | tf_op | source)
XLA Modules:
  0.0 54.1 jit_solution(4624223765846551367)
XLA Ops:
  0.0 0.7 %pad_add_fusion.ids = s32[4,128]{1,0:T(4,128)S(1)} fusion(s32[1,128]{1,0:T(1,128)} %bitcast.9, s32[1,128]{1,0:T(1,128)} %bitcast.10, s32[1,128]{1,0:T(1,128)} %bitcast.11, s32[1,128]{1,0:T(1,128)} %bitcast.12), kind=kLoop, calls=%fused_computation | loop fusion | flops 1536 | bytes 4096 | tf_op jit(solution)/shard_map/stack | solution.py:395
  0.7 0.0 copy-start.1
  0.7 1.0 %copy-done.1 = f32[8,64,256]{2,1,0:T(8,128)S(1)} copy-done((f32[8,64,256]{2,1,0:T(8,128)S(1)}, f32[8,64,256]{2,1,0:T(8,128)}, u32[]{:S(2)}) %copy-start.1) | copy-done | bytes 524312
  1.8 0.0 copy-start.2
  1.8 0.7 %copy-done.2 = f32[32,128]{1,0:T(8,128)S(1)} copy-done((f32[32,128]{1,0:T(8,128)S(1)}, f32[32,128]{1,0:T(8,128)}, u32[]{:S(2)}) %copy-start.2) | copy-done | bytes 16408
  2.5 0.5 %prepare.1 = (f32[48,128]{1,0:T(8,128)S(1)}, f32[48,128]{1,0:T(8,128)S(1)}, f32[40,128]{1,0:T(8,128)S(1)}, f32[40,128]{1,0:T(8,128)S(1)}, s32[24,128]{1,0:T(8,12...) custom-call(f32[512,256]{1,0:T(8,128)S(1)} %bitcast.8, f32[32,128]{1,0:T(8,128)S(1)} %copy-done.2, ...), custom_call_target="tpu_custom_call" | custom-call | tf_op jit(solution)/shard_map/prepare/pallas_call | solution.py:397
  3.0 0.1 collective-permute-start
  3.1 3.0 %collective-permute-start.1 = (f32[48,128]{1,0:T(8,128)S(1)}, f32[48,128]{1,0:T(8,128)S(1)}, u32[]{:S(2)}, u32[]{:S(2)}) collective-permute-start(f32[48,128]{1,0:T(8,128)S(1)} %get-tuple-element.20), channel_id=1, source_target_pairs={{0,112},{16,32},{32,16},{48,64},{64,48},{80,96},{96,80},{112,0},{1... | collective-permute-start | bytes 73736 | tf_op jit(solution)/shard_map/ppermute | solution.py:411
  6.1 1.9 %collective-permute-start.2 = (f32[40,128]{1,0:T(8,128)S(1)}, f32[40,128]{1,0:T(8,128)S(1)}, u32[]{:S(2)}, u32[]{:S(2)}) collective-permute-start(f32[40,128]{1,0:T(8,128)S(1)} %get-tuple-element.21), channel_id=1, source_target_pairs={{0,1},{1,0},{2,3},{3,2},{4,5},{5,4},{6,7},{7,6},{8,9},{9,8},{10,11... | collective-permute-start | bytes 61448 | tf_op jit(solution)/shard_map/ppermute | solution.py:411
  8.0 5.0 %collective-permute-start.3 = (f32[40,128]{1,0:T(8,128)S(1)}, f32[40,128]{1,0:T(8,128)S(1)}, u32[]{:S(2)}, u32[]{:S(2)}) collective-permute-start(f32[40,128]{1,0:T(8,128)S(1)} %get-tuple-element.22), channel_id=1, source_target_pairs={{0,15},{1,2},{2,1},{3,4},{4,3},{5,6},{6,5},{7,8},{8,7},{9,10},{10,... | collective-permute-start | bytes 61448 | tf_op jit(solution)/shard_map/ppermute | solution.py:411
  13.0 0.0 copy-start
  13.0 1.9 %copy-done = bf16[16,3,256,128]{3,2,1,0:T(8,128)(2,1)S(1)} copy-done((bf16[16,3,256,128]{3,2,1,0:T(8,128)(2,1)S(1)}, bf16[16,3,256,128]{3,2,1,0:T(8,128)(2,1)}, u32[]{:S(2)}) %copy-start) | copy-done | bytes 3145752
  14.9 3.3 %tiles.1 = (bf16[512,768]{1,0:T(8,128)(2,1)S(1)}, f32[128,128]{1,0:T(8,128)S(1)}, bf16[16,768,128]{2,1,0:T(8,128)(2,1)S(1)}) custom-call(f32[2,512,128]{2,1,0:T(8,128)S(1)} %get-tuple-element.16.flux, s32[24,128]{1,0:T(8,128)S(1)} %get-tuple-element.15.tabv.tab_in, bf16[16,768,128]{2,1,0:T(8,128)(2,1)S(1)} %bitcast.7), custom_call_target="tpu_custom_call" | custom-call | tf_op jit(solution)/shard_map/tiles/pallas_call | solution.py:418
  18.1 0.0 collective-permute-done.2.from_a
  18.2 0.0 collective-permute-done.3.from_b
  18.2 0.0 collective-permute-done.from_c
  18.2 0.0 collective-permute-done.1.from_x
  18.2 5.0 %remap_send.1 = bf16[128,3,16,128]{3,2,1,0:T(8,128)(2,1)S(1)} custom-call(s32[24,128]{1,0:T(8,128)S(1)} %get-tuple-element.15.tabv.tab_in, bf16[512,768]{1,0:T(8,128)(2,1)S(1)} %get-tuple-element.17.lhs_in, f32[128,128]{1,0:T(8,128)S(1)} %get-tuple-element.18.lab, f32[48,128]{1,0:T(8,128)S(1)} %collective-permute-done.from_c, ...), custom_call_target="tpu_custom_call" | custom-call | tf_op jit(solution)/shard_map/remap_send/pallas_call | solution.py:429
  23.2 28.5 %all_to_all.5.recv = bf16[128,3,16,128]{3,2,1,0:T(8,128)(2,1)S(1)} all-to-all(bf16[128,3,16,128]{3,2,1,0:T(8,128)(2,1)S(1)} %remap_send.1), channel_id=1, replica_groups=mesh['gx'=8,'gy'=16] {'gx','gy'}, dimensions={0} | all-to-all | bytes 3145728 | tf_op jit(solution)/shard_map/all_to_all | solution.py:447
  51.6 2.4 %ocean.1 = f32[256,128]{1,0:T(8,128)} custom-call(bf16[128,3,16,128]{3,2,1,0:T(8,128)(2,1)S(1)} %all_to_all.5.recv, f32[32,128]{1,0:T(8,128)S(1)} %get-tuple-element.23.diff, f32[48,128]{1,0:T(8,128)S(1)} %collective-permute-done.from_c, f32[48,128]{1,0:T(8,128)S(1)} %collective-permute-done.1.from_x, f32[40,128]{1,0:T(8,128)S(1)} %collective-permute-done.2.from_a, ...), custom_call_target="tpu_custom_call" | custom-call | tf_op jit(solution)/shard_map/ocean/pallas_call | solution.py:448
Async XLA Ops:
  0.7 1.0 %copy-start.1 = (f32[8,64,256]{2,1,0:T(8,128)S(1)}, f32[8,64,256]{2,1,0:T(8,128)}, u32[]{:S(2)}) copy-start(f32[8,64,256]{2,1,0:T(8,128)} %param.7) | copy-start | bytes 1572868
  1.8 0.7 %copy-start.2 = (f32[32,128]{1,0:T(8,128)S(1)}, f32[32,128]{1,0:T(8,128)}, u32[]{:S(2)}) copy-start(f32[32,128]{1,0:T(8,128)} %diff_in.1) | copy-start | bytes 49156
  3.0 15.1 %collective-permute-start = (f32[48,128]{1,0:T(8,128)S(1)}, f32[48,128]{1,0:T(8,128)S(1)}, u32[]{:S(2)}, u32[]{:S(2)}) collective-permute-start(f32[48,128]{1,0:T(8,128)S(1)} %get-tuple-element.19), channel_id=1, source_target_pairs={{0,16},{16,0},{32,48},{48,32},{64,80},{80,64},{96,112},{112,96},{1... | collective-permute-start | bytes 73736 | tf_op jit(solution)/shard_map/ppermute | solution.py:411
  3.1 15.1 %collective-permute-start.1 = (f32[48,128]{1,0:T(8,128)S(1)}, f32[48,128]{1,0:T(8,128)S(1)}, u32[]{:S(2)}, u32[]{:S(2)}) collective-permute-start(f32[48,128]{1,0:T(8,128)S(1)} %get-tuple-element.20), channel_id=1, source_target_pairs={{0,112},{16,32},{32,16},{48,64},{64,48},{80,96},{96,80},{112,0},{1... | collective-permute-start | bytes 73736 | tf_op jit(solution)/shard_map/ppermute | solution.py:411
  6.1 12.1 %collective-permute-start.2 = (f32[40,128]{1,0:T(8,128)S(1)}, f32[40,128]{1,0:T(8,128)S(1)}, u32[]{:S(2)}, u32[]{:S(2)}) collective-permute-start(f32[40,128]{1,0:T(8,128)S(1)} %get-tuple-element.21), channel_id=1, source_target_pairs={{0,1},{1,0},{2,3},{3,2},{4,5},{5,4},{6,7},{7,6},{8,9},{9,8},{10,11... | collective-permute-start | bytes 61448 | tf_op jit(solution)/shard_map/ppermute | solution.py:411
  8.0 10.1 %collective-permute-start.3 = (f32[40,128]{1,0:T(8,128)S(1)}, f32[40,128]{1,0:T(8,128)S(1)}, u32[]{:S(2)}, u32[]{:S(2)}) collective-permute-start(f32[40,128]{1,0:T(8,128)S(1)} %get-tuple-element.22), channel_id=1, source_target_pairs={{0,15},{1,2},{2,1},{3,4},{4,3},{5,6},{6,5},{7,8},{8,7},{9,10},{10,... | collective-permute-start | bytes 61448 | tf_op jit(solution)/shard_map/ppermute | solution.py:411
  13.0 1.9 %copy-start = (bf16[16,3,256,128]{3,2,1,0:T(8,128)(2,1)S(1)}, bf16[16,3,256,128]{3,2,1,0:T(8,128)(2,1)}, u32[]{:S(2)}) copy-start(bf16[16,3,256,128]{3,2,1,0:T(8,128)(2,1)} %param.9) | copy-start | bytes 9437188

commit v5 on v4

--- a/solution.py
+++ b/solution.py
@@ -62,13 +62,16 @@
     )
 
 
-def prepare_kernel(flux_in, diff_in, ids, to_c, to_x, to_a, to_b, tab, flux, diff, sems):
-    moves = [(diff_in, diff)] + [(flux_in.at[:, pl.ds(g * 128, 128)], flux.at[g]) for g in range(2)]
+def prepare_kernel(flux_in, diff_in, owner_in, source_in, target_in, weight_in, to_c, to_x, to_a, to_b, tab, flux, diff, ids, sems):
+    moves = [(x, ids.at[n]) for n, x in enumerate((owner_in, source_in, target_in, weight_in))]
+    moves += [(diff_in, diff)] + [(flux_in.at[:, pl.ds(g * 128, 128)], flux.at[g]) for g in range(2)]
     copies = [pltpu.make_async_copy(src, dst, sems.at[n]) for n, (src, dst) in enumerate(moves)]
     for copy in copies:
         copy.start()
     lane = lanes((8, 128))
-    owner, source, target, weight = (ids[n : n + 1, :] for n in range(4))
+    for copy in copies[:5]:
+        copy.wait()
+    owner, source, target, weight = (ids[n] for n in range(4))
     across = jnp.broadcast_to(owner, (RECS, RECS))
     along = jnp.transpose(across.astype(jnp.float32)).astype(jnp.int32)
     sub = lax.broadcasted_iota(jnp.int32, (RECS, RECS), 0)
@@ -98,12 +101,11 @@
     for n in range(len(rows), TAB_ROWS):
         tab[n : n + 1, :] = slot
 
-    copies[0].wait()
     for to in (to_c, to_x):
         to[16:48, :] = diff[...]
     for to in (to_a, to_b):
         to[8:40, :] = diff[...]
-    for copy in copies[1:]:
+    for copy in copies[5:]:
         copy.wait()
 
     def row(i, g):
@@ -232,7 +234,7 @@
         prod[pl.ds(at + 512, 512), :] = res[:, 128:]
         return carry
 
-    lax.fori_loop(0, NWB // 2, product, 0)
+    lax.fori_loop(0, NWB // 2, product, 0, unroll=4)
 
     half_of, quarter_of = lane // 64, b_of // 4
     code = half_of * 4 + quarter_of
@@ -392,7 +394,8 @@
     anywhere = pl.BlockSpec(memory_space=pl.ANY)
     flux_rows = flux.reshape(F * AXD, AYD)
     hbm = pl.BlockSpec(memory_space=pltpu.HBM)
-    records = jnp.stack([rec_owner, rec_source, rec_target, rec_weight])
+    records = [x.reshape(1, RECS) for x in (rec_owner, rec_source, rec_target, rec_weight)]
+    loads = [pltpu.with_memory_space_constraint(x, pltpu.HBM) for x in (flux_rows, diffusivity, *records)]
     f32, i32 = jnp.float32, jnp.int32
     to_c, to_x, to_a, to_b, tab, flux_halves, diff = pl.pallas_call(
         prepare_kernel,
@@ -400,12 +403,13 @@
         + [jax.ShapeDtypeStruct((40, 128), f32)] * 2
         + [jax.ShapeDtypeStruct((TAB_ROWS, RECS), i32), jax.ShapeDtypeStruct((2, F * AXD, 128), f32)]
         + [jax.ShapeDtypeStruct((OXD, OYD), f32)],
-        in_specs=[hbm] * 2 + [vmem],
+        in_specs=[hbm] * 6,
         out_specs=[vmem] * 7,
-        scratch_shapes=[pltpu.SemaphoreType.DMA((3,))],
+        scratch_shapes=[pltpu.VMEM((4, 1, RECS), i32), pltpu.SemaphoreType.DMA((7,))],
         name="prepare",
+        cost_estimate=pl.CostEstimate(flops=3000000000, bytes_accessed=8000000, transcendentals=0),
         compiler_params=pltpu.CompilerParams(vmem_limit_bytes=6 << 20),
-    )(flux_rows, diffusivity, records)
+    )(*loads)
 
     def swap(x, axis, count, odd):
         return lax.ppermute(x, axis, [(i, (((i + odd) ^ 1) - odd) % count) for i in range(count)])
@@ -423,6 +427,7 @@
         out_specs=[vmem] * 3,
         scratch_shapes=[pltpu.SemaphoreType.DMA],
         name="tiles",
+    cost_estimate=pl.CostEstimate(flops=3000000000, bytes_accessed=8000000, transcendentals=0),
     compiler_params=pltpu.CompilerParams(vmem_limit_bytes=8 << 20),
     )(flux_halves, tab, remap_bank.reshape(NWB, 768, 128))
 
@@ -442,6 +447,7 @@
             pltpu.SemaphoreType.DMA((2,)),
         ],
         name="remap_send",
+        cost_estimate=pl.CostEstimate(flops=5000000000, bytes_accessed=8000000, transcendentals=0),
         compiler_params=pltpu.CompilerParams(vmem_limit_bytes=24 << 20),
     )(tab, lhs, lab, *came, diff, bank)
     arrived = lax.all_to_all(outgoing, ("gx", "gy"), split_axis=0, concat_axis=0, tiled=True)
@@ -457,6 +463,7 @@
             pltpu.VMEM((40, 8, 256), f32),
         ],
         name="ocean",
+        cost_estimate=pl.CostEstimate(flops=3000000000, bytes_accessed=4000000, transcendentals=0),
         compiler_params=pltpu.CompilerParams(vmem_limit_bytes=16 << 20),
     )(arrived, diff, *came)
     return ocean.reshape(F, OXD, OYD)

time: 54.4 us -> 51.1 us (0.939)
  local copies, waits for them, and re-layouts: 3.65 us -> 0.01 us
  blocking collectives: 28.5 us -> 29.6 us
  other arithmetic: 0.71 us -> 0 us
    unnamed x6 -> x2, local copies, waits for them, and re-layouts: 3.65 us -> 0.01 us
    all_to_all x1, blocking collectives: 28.5 us -> 29.6 us  [local(): lax.all_to_all(outgoing, ('gx', 'gy'), split_axis=0, concat_axis=0, tiled...]
    pallas_call x1, Pallas kernels: 0.55 us -> 1.67 us  [local(): pl.pallas_call(prepare_kernel, out_shape=[jax.ShapeDtypeStruct((48, 128),...]
    pallas_call x1, Pallas kernels: 4.96 us -> 3.92 us  [local(): pl.pallas_call(send_kernel, out_shape=jax.ShapeDtypeStruct((OWNERS, 3, 16...]
    another operation x1 -> x0, other arithmetic: 0.71 us -> none  [local(): records = jnp.stack([rec_owner, rec_source, rec_target, rec_weight])]
where the time goes in v5:
time: 51.1 us; the launch traced here: 50.9 us
  blocking collectives  29.6 us (58%)
  Pallas kernels  11.3 us (22%)
  starting transfers between devices  9.95 us (19%)
    all_to_all x1, blocking collectives, local(): lax.all_to_all(outgoing, ('gx', 'gy'), split_axis=0, concat_axis=0, tiled...  29.6 us
    ppermute x4, starting transfers between devices, swap(): lax.ppermute(x, axis, [(i, ((i + odd ^ 1) - odd) % count) for i in range(...  9.95 us
    pallas_call x1, Pallas kernels, local(): pl.pallas_call(send_kernel, out_shape=jax.ShapeDtypeStruct((OWNERS, 3, 16...  3.92 us
    pallas_call x1, Pallas kernels, local(): pl.pallas_call(tiles_kernel, out_shape=[jax.ShapeDtypeStruct((512, 768),...  3.26 us
    pallas_call x1, Pallas kernels, local(): pl.pallas_call(ocean_kernel, out_shape=jax.ShapeDtypeStruct((F * OXD, OYD...  2.44 us
    pallas_call x1, Pallas kernels, local(): pl.pallas_call(prepare_kernel, out_shape=[jax.ShapeDtypeStruct((48, 128),...  1.67 us
  transfers between devices with their start and end apart: 4, of which 0 were waited for; matrix products, arithmetic and copies ran while one was open for 0% of the time, Pallas kernels for 6%

profile of v5, /device:TPU:0, one launch (start us, length us, event | category | flops | bytes accessed | tf_op | source)
XLA Modules:
  0.0 50.9 jit_solution(10394905435750239194)
XLA Ops:
  0.0 0.0 copy-start
  0.0 1.7 %prepare.1 = (f32[48,128]{1,0:T(8,128)S(1)}, f32[48,128]{1,0:T(8,128)S(1)}, f32[40,128]{1,0:T(8,128)S(1)}, f32[40,128]{1,0:T(8,128)S(1)}, s32[24,128]{1,0:T(8,12...) custom-call(f32[512,256]{1,0:T(8,128)} %bitcast.8, f32[32,128]{1,0:T(8,128)} %diff_in.1, s32[1,128]{1,0:T(1,128)} %bitcast.9, ...), custom_call_target="tpu_custom_call" | custom-call | flops 3000000000 | bytes 8000000 | tf_op jit(solution)/shard_map/prepare/pallas_call | solution.py:400
  1.7 2.1 %collective-permute-start.2 = (f32[40,128]{1,0:T(8,128)S(1)}, f32[40,128]{1,0:T(8,128)S(1)}, u32[]{:S(2)}, u32[]{:S(2)}) collective-permute-start(f32[40,128]{1,0:T(8,128)S(1)} %get-tuple-element.21), channel_id=1, source_target_pairs={{0,1},{1,0},{2,3},{3,2},{4,5},{5,4},{6,7},{7,6},{8,9},{9,8},{10,11... | collective-permute-start | bytes 61448 | tf_op jit(solution)/shard_map/ppermute | solution.py:415
  3.8 5.0 %collective-permute-start.3 = (f32[40,128]{1,0:T(8,128)S(1)}, f32[40,128]{1,0:T(8,128)S(1)}, u32[]{:S(2)}, u32[]{:S(2)}) collective-permute-start(f32[40,128]{1,0:T(8,128)S(1)} %get-tuple-element.22), channel_id=1, source_target_pairs={{0,15},{1,2},{2,1},{3,4},{4,3},{5,6},{6,5},{7,8},{8,7},{9,10},{10,... | collective-permute-start | bytes 61448 | tf_op jit(solution)/shard_map/ppermute | solution.py:415
  8.8 0.0 collective-permute-start
  8.8 2.9 %collective-permute-start.1 = (f32[48,128]{1,0:T(8,128)S(1)}, f32[48,128]{1,0:T(8,128)S(1)}, u32[]{:S(2)}, u32[]{:S(2)}) collective-permute-start(f32[48,128]{1,0:T(8,128)S(1)} %get-tuple-element.20), channel_id=1, source_target_pairs={{0,112},{16,32},{32,16},{48,64},{64,48},{80,96},{96,80},{112,0},{1... | collective-permute-start | bytes 73736 | tf_op jit(solution)/shard_map/ppermute | solution.py:415
  11.6 0.0 copy-done
  11.6 3.3 %tiles.1 = (bf16[512,768]{1,0:T(8,128)(2,1)S(1)}, f32[128,128]{1,0:T(8,128)S(1)}, bf16[16,768,128]{2,1,0:T(8,128)(2,1)S(1)}) custom-call(f32[2,512,128]{2,1,0:T(8,128)S(1)} %get-tuple-element.16.flux, s32[24,128]{1,0:T(8,128)S(1)} %get-tuple-element.15.tabv.tab_in, bf16[16,768,128]{2,1,0:T(8,128)(2,1)S(1)} %bitcast.7), custom_call_target="tpu_custom_call" | custom-call | flops 3000000000 | bytes 8000000 | tf_op jit(solution)/shard_map/tiles/pallas_call | solution.py:422
  14.9 0.0 collective-permute-done.2.from_a
  14.9 0.0 collective-permute-done.3.from_b
  14.9 0.0 collective-permute-done.from_c
  14.9 0.0 collective-permute-done.1.from_x
  15.0 3.9 %remap_send.1 = bf16[128,3,16,128]{3,2,1,0:T(8,128)(2,1)S(1)} custom-call(s32[24,128]{1,0:T(8,128)S(1)} %get-tuple-element.15.tabv.tab_in, bf16[512,768]{1,0:T(8,128)(2,1)S(1)} %get-tuple-element.17.lhs_in, f32[128,128]{1,0:T(8,128)S(1)} %get-tuple-element.18.lab, f32[48,128]{1,0:T(8,128)S(1)} %collective-permute-done.from_c, ...), custom_call_target="tpu_custom_call" | custom-call | flops 5000000000 | bytes 8000000 | tf_op jit(solution)/shard_map/remap_send/pallas_call | solution.py:434
  18.9 29.6 %all_to_all.5.recv = bf16[128,3,16,128]{3,2,1,0:T(8,128)(2,1)S(1)} all-to-all(bf16[128,3,16,128]{3,2,1,0:T(8,128)(2,1)S(1)} %remap_send.1), channel_id=1, replica_groups=mesh['gx'=8,'gy'=16] {'gx','gy'}, dimensions={0} | all-to-all | bytes 3145728 | tf_op jit(solution)/shard_map/all_to_all | solution.py:453
  48.5 2.4 %ocean.1 = f32[256,128]{1,0:T(8,128)} custom-call(bf16[128,3,16,128]{3,2,1,0:T(8,128)(2,1)S(1)} %all_to_all.5.recv, f32[32,128]{1,0:T(8,128)S(1)} %get-tuple-element.23.diff, f32[48,128]{1,0:T(8,128)S(1)} %collective-permute-done.from_c, f32[48,128]{1,0:T(8,128)S(1)} %collective-permute-done.1.from_x, f32[40,128]{1,0:T(8,128)S(1)} %collective-permute-done.2.from_a, ...), custom_call_target="tpu_custom_call" | custom-call | flops 3000000000 | bytes 4000000 | tf_op jit(solution)/shard_map/ocean/pallas_call | solution.py:454
Async XLA Ops:
  0.0 11.6 %copy-start = (bf16[16,3,256,128]{3,2,1,0:T(8,128)(2,1)S(1)}, bf16[16,3,256,128]{3,2,1,0:T(8,128)(2,1)}, u32[]{:S(2)}) copy-start(bf16[16,3,256,128]{3,2,1,0:T(8,128)(2,1)} %param.9) | copy-start | bytes 9437188
  1.7 13.2 %collective-permute-start.2 = (f32[40,128]{1,0:T(8,128)S(1)}, f32[40,128]{1,0:T(8,128)S(1)}, u32[]{:S(2)}, u32[]{:S(2)}) collective-permute-start(f32[40,128]{1,0:T(8,128)S(1)} %get-tuple-element.21), channel_id=1, source_target_pairs={{0,1},{1,0},{2,3},{3,2},{4,5},{5,4},{6,7},{7,6},{8,9},{9,8},{10,11... | collective-permute-start | bytes 61448 | tf_op jit(solution)/shard_map/ppermute | solution.py:415
  3.8 11.1 %collective-permute-start.3 = (f32[40,128]{1,0:T(8,128)S(1)}, f32[40,128]{1,0:T(8,128)S(1)}, u32[]{:S(2)}, u32[]{:S(2)}) collective-permute-start(f32[40,128]{1,0:T(8,128)S(1)} %get-tuple-element.22), channel_id=1, source_target_pairs={{0,15},{1,2},{2,1},{3,4},{4,3},{5,6},{6,5},{7,8},{8,7},{9,10},{10,... | collective-permute-start | bytes 61448 | tf_op jit(solution)/shard_map/ppermute | solution.py:415
  8.8 6.2 %collective-permute-start = (f32[48,128]{1,0:T(8,128)S(1)}, f32[48,128]{1,0:T(8,128)S(1)}, u32[]{:S(2)}, u32[]{:S(2)}) collective-permute-start(f32[48,128]{1,0:T(8,128)S(1)} %get-tuple-element.19), channel_id=1, source_target_pairs={{0,16},{16,0},{32,48},{48,32},{64,80},{80,64},{96,112},{112,96},{1... | collective-permute-start | bytes 73736 | tf_op jit(solution)/shard_map/ppermute | solution.py:415
  8.8 6.2 %collective-permute-start.1 = (f32[48,128]{1,0:T(8,128)S(1)}, f32[48,128]{1,0:T(8,128)S(1)}, u32[]{:S(2)}, u32[]{:S(2)}) collective-permute-start(f32[48,128]{1,0:T(8,128)S(1)} %get-tuple-element.20), channel_id=1, source_target_pairs={{0,112},{16,32},{32,16},{48,64},{64,48},{80,96},{96,80},{112,0},{1... | collective-permute-start | bytes 73736 | tf_op jit(solution)/shard_map/ppermute | solution.py:415

commit v6 on v5

--- a/solution.py
+++ b/solution.py
@@ -125,9 +125,7 @@
     to_b[0:8, :] = jnp.where(even_y, first, last)
 
 
-def tiles_kernel(flux, tabv, bank_in, lhs, lab, bank, sem):
-    weights = pltpu.make_async_copy(bank_in, bank, sem)
-    weights.start()
+def tiles_kernel(flux, tabv, lhs, lab):
     rows3 = lax.broadcasted_iota(jnp.int32, (128, 3 * RECS), 0)
 
     def three(*at):
@@ -165,7 +163,6 @@
                 ]
                 for q, tile in enumerate(swap_blocks(packed)):
                     lhs[pl.ds((ti * 8 + q) * 16, 16), pl.ds(k * 256 + h * 128, 128)] = tile
-    weights.wait()
 
 
 def send_kernel(
@@ -234,7 +231,7 @@
         prod[pl.ds(at + 512, 512), :] = res[:, 128:]
         return carry
 
-    lax.fori_loop(0, NWB // 2, product, 0, unroll=4)
+    lax.fori_loop(0, NWB // 2, product, 0, unroll=8)
 
     half_of, quarter_of = lane // 64, b_of // 4
     code = half_of * 4 + quarter_of
@@ -419,17 +416,15 @@
         came.append(swap(x, axis, count, odd))
 
     bf16 = jnp.bfloat16
-    lhs, lab, bank = pl.pallas_call(
+    lhs, lab = pl.pallas_call(
         tiles_kernel,
-        out_shape=[jax.ShapeDtypeStruct((512, 768), bf16), jax.ShapeDtypeStruct((OWNERS, 128), f32)]
-        + [jax.ShapeDtypeStruct((NWB, 768, 128), bf16)],
-        in_specs=[vmem, vmem, hbm],
-        out_specs=[vmem] * 3,
-        scratch_shapes=[pltpu.SemaphoreType.DMA],
+        out_shape=[jax.ShapeDtypeStruct((512, 768), bf16), jax.ShapeDtypeStruct((OWNERS, 128), f32)],
+        in_specs=[vmem] * 2,
+        out_specs=[vmem] * 2,
         name="tiles",
     cost_estimate=pl.CostEstimate(flops=3000000000, bytes_accessed=8000000, transcendentals=0),
     compiler_params=pltpu.CompilerParams(vmem_limit_bytes=8 << 20),
-    )(flux_halves, tab, remap_bank.reshape(NWB, 768, 128))
+    )(flux_halves, tab)
 
     outgoing = pl.pallas_call(
         send_kernel,
@@ -449,7 +444,7 @@
         name="remap_send",
         cost_estimate=pl.CostEstimate(flops=5000000000, bytes_accessed=8000000, transcendentals=0),
         compiler_params=pltpu.CompilerParams(vmem_limit_bytes=24 << 20),
-    )(tab, lhs, lab, *came, diff, bank)
+    )(tab, lhs, lab, *came, diff, remap_bank.reshape(NWB, 768, 128))
     arrived = lax.all_to_all(outgoing, ("gx", "gy"), split_axis=0, concat_axis=0, tiled=True)
     ocean = pl.pallas_call(
         ocean_kernel,

time: 51.1 us -> 50.5 us (0.988)
  Pallas kernels: 11.3 us -> 10.5 us
where the time goes in v6:
time: 50.5 us; the launch traced here: 50.4 us
  blocking collectives  29.8 us (59%)
  Pallas kernels  10.5 us (21%)
  starting transfers between devices  9.95 us (20%)
    all_to_all x1, blocking collectives, local(): lax.all_to_all(outgoing, ('gx', 'gy'), split_axis=0, concat_axis=0, tiled...  29.8 us
    ppermute x4, starting transfers between devices, swap(): lax.ppermute(x, axis, [(i, ((i + odd ^ 1) - odd) % count) for i in range(...  9.95 us
    pallas_call x1, Pallas kernels, local(): pl.pallas_call(send_kernel, out_shape=jax.ShapeDtypeStruct((OWNERS, 3, 16...  3.48 us
    pallas_call x1, Pallas kernels, local(): pl.pallas_call(tiles_kernel, out_shape=[jax.ShapeDtypeStruct((512, 768),...  3.04 us
    pallas_call x1, Pallas kernels, local(): pl.pallas_call(ocean_kernel, out_shape=jax.ShapeDtypeStruct((F * OXD, OYD...  2.44 us
    pallas_call x1, Pallas kernels, local(): pl.pallas_call(prepare_kernel, out_shape=[jax.ShapeDtypeStruct((48, 128),...  1.52 us
  transfers between devices with their start and end apart: 4, of which 0 were waited for; matrix products, arithmetic and copies ran while one was open for 0% of the time, Pallas kernels for 6%

profile of v6, /device:TPU:0, one launch (start us, length us, event | category | flops | bytes accessed | tf_op | source)
XLA Modules:
  0.0 50.4 jit_solution(14877071573186525828)
XLA Ops:
  0.0 1.5 %prepare.1 = (f32[48,128]{1,0:T(8,128)S(1)}, f32[48,128]{1,0:T(8,128)S(1)}, f32[40,128]{1,0:T(8,128)S(1)}, f32[40,128]{1,0:T(8,128)S(1)}, s32[24,128]{1,0:T(8,12...) custom-call(f32[512,256]{1,0:T(8,128)} %bitcast.8, f32[32,128]{1,0:T(8,128)} %diff_in.1, s32[1,128]{1,0:T(1,128)} %bitcast.9, ...), custom_call_target="tpu_custom_call" | custom-call | flops 3000000000 | bytes 8000000 | tf_op jit(solution)/shard_map/prepare/pallas_call | solution.py:397
  1.5 2.1 %collective-permute-start.2 = (f32[40,128]{1,0:T(8,128)S(1)}, f32[40,128]{1,0:T(8,128)S(1)}, u32[]{:S(2)}, u32[]{:S(2)}) collective-permute-start(f32[40,128]{1,0:T(8,128)S(1)} %get-tuple-element.20), channel_id=1, source_target_pairs={{0,1},{1,0},{2,3},{3,2},{4,5},{5,4},{6,7},{7,6},{8,9},{9,8},{10,11... | collective-permute-start | bytes 61448 | tf_op jit(solution)/shard_map/ppermute | solution.py:412
  3.6 5.0 %collective-permute-start.3 = (f32[40,128]{1,0:T(8,128)S(1)}, f32[40,128]{1,0:T(8,128)S(1)}, u32[]{:S(2)}, u32[]{:S(2)}) collective-permute-start(f32[40,128]{1,0:T(8,128)S(1)} %get-tuple-element.21), channel_id=1, source_target_pairs={{0,15},{1,2},{2,1},{3,4},{4,3},{5,6},{6,5},{7,8},{8,7},{9,10},{10,... | collective-permute-start | bytes 61448 | tf_op jit(solution)/shard_map/ppermute | solution.py:412
  8.6 0.0 collective-permute-start
  8.6 2.9 %collective-permute-start.1 = (f32[48,128]{1,0:T(8,128)S(1)}, f32[48,128]{1,0:T(8,128)S(1)}, u32[]{:S(2)}, u32[]{:S(2)}) collective-permute-start(f32[48,128]{1,0:T(8,128)S(1)} %get-tuple-element.19), channel_id=1, source_target_pairs={{0,112},{16,32},{32,16},{48,64},{64,48},{80,96},{96,80},{112,0},{1... | collective-permute-start | bytes 73736 | tf_op jit(solution)/shard_map/ppermute | solution.py:412
  11.5 0.0 copy-start
  11.5 3.0 %tiles.1 = (bf16[512,768]{1,0:T(8,128)(2,1)S(1)}, f32[128,128]{1,0:T(8,128)S(1)}) custom-call(f32[2,512,128]{2,1,0:T(8,128)S(1)} %get-tuple-element.15.flux, s32[24,128]{1,0:T(8,128)S(1)} %get-tuple-element.14.tabv.tab_in), custom_call_target="tpu_custom_call" | custom-call | flops 3000000000 | bytes 8000000 | tf_op jit(solution)/shard_map/tiles/pallas_call | solution.py:419
  14.5 0.0 collective-permute-done.2.from_a
  14.5 0.0 collective-permute-done.3.from_b
  14.6 0.0 collective-permute-done.from_c
  14.6 0.0 collective-permute-done.1.from_x
  14.6 0.0 copy-done
  14.6 3.5 %remap_send.1 = bf16[128,3,16,128]{3,2,1,0:T(8,128)(2,1)S(1)} custom-call(s32[24,128]{1,0:T(8,128)S(1)} %get-tuple-element.14.tabv.tab_in, bf16[512,768]{1,0:T(8,128)(2,1)S(1)} %get-tuple-element.16.lhs_in, f32[128,128]{1,0:T(8,128)S(1)} %get-tuple-element.17.lab, f32[48,128]{1,0:T(8,128)S(1)} %collective-permute-done.from_c, ...), custom_call_target="tpu_custom_call" | custom-call | flops 5000000000 | bytes 8000000 | tf_op jit(solution)/shard_map/remap_send/pallas_call | solution.py:429
  18.1 29.8 %all_to_all.5.recv = bf16[128,3,16,128]{3,2,1,0:T(8,128)(2,1)S(1)} all-to-all(bf16[128,3,16,128]{3,2,1,0:T(8,128)(2,1)S(1)} %remap_send.1), channel_id=1, replica_groups=mesh['gx'=8,'gy'=16] {'gx','gy'}, dimensions={0} | all-to-all | bytes 3145728 | tf_op jit(solution)/shard_map/all_to_all | solution.py:448
  47.9 2.4 %ocean.1 = f32[256,128]{1,0:T(8,128)} custom-call(bf16[128,3,16,128]{3,2,1,0:T(8,128)(2,1)S(1)} %all_to_all.5.recv, f32[32,128]{1,0:T(8,128)S(1)} %get-tuple-element.22.diff, f32[48,128]{1,0:T(8,128)S(1)} %collective-permute-done.from_c, f32[48,128]{1,0:T(8,128)S(1)} %collective-permute-done.1.from_x, f32[40,128]{1,0:T(8,128)S(1)} %collective-permute-done.2.from_a, ...), custom_call_target="tpu_custom_call" | custom-call | flops 3000000000 | bytes 4000000 | tf_op jit(solution)/shard_map/ocean/pallas_call | solution.py:449
Async XLA Ops:
  1.5 13.0 %collective-permute-start.2 = (f32[40,128]{1,0:T(8,128)S(1)}, f32[40,128]{1,0:T(8,128)S(1)}, u32[]{:S(2)}, u32[]{:S(2)}) collective-permute-start(f32[40,128]{1,0:T(8,128)S(1)} %get-tuple-element.20), channel_id=1, source_target_pairs={{0,1},{1,0},{2,3},{3,2},{4,5},{5,4},{6,7},{7,6},{8,9},{9,8},{10,11... | collective-permute-start | bytes 61448 | tf_op jit(solution)/shard_map/ppermute | solution.py:412
  3.6 10.9 %collective-permute-start.3 = (f32[40,128]{1,0:T(8,128)S(1)}, f32[40,128]{1,0:T(8,128)S(1)}, u32[]{:S(2)}, u32[]{:S(2)}) collective-permute-start(f32[40,128]{1,0:T(8,128)S(1)} %get-tuple-element.21), channel_id=1, source_target_pairs={{0,15},{1,2},{2,1},{3,4},{4,3},{5,6},{6,5},{7,8},{8,7},{9,10},{10,... | collective-permute-start | bytes 61448 | tf_op jit(solution)/shard_map/ppermute | solution.py:412
  8.6 5.9 %collective-permute-start = (f32[48,128]{1,0:T(8,128)S(1)}, f32[48,128]{1,0:T(8,128)S(1)}, u32[]{:S(2)}, u32[]{:S(2)}) collective-permute-start(f32[48,128]{1,0:T(8,128)S(1)} %get-tuple-element.18), channel_id=1, source_target_pairs={{0,16},{16,0},{32,48},{48,32},{64,80},{80,64},{96,112},{112,96},{1... | collective-permute-start | bytes 73736 | tf_op jit(solution)/shard_map/ppermute | solution.py:412
  8.6 5.9 %collective-permute-start.1 = (f32[48,128]{1,0:T(8,128)S(1)}, f32[48,128]{1,0:T(8,128)S(1)}, u32[]{:S(2)}, u32[]{:S(2)}) collective-permute-start(f32[48,128]{1,0:T(8,128)S(1)} %get-tuple-element.19), channel_id=1, source_target_pairs={{0,112},{16,32},{32,16},{48,64},{64,48},{80,96},{96,80},{112,0},{1... | collective-permute-start | bytes 73736 | tf_op jit(solution)/shard_map/ppermute | solution.py:412
  11.5 3.1 %copy-start = (bf16[16,3,256,128]{3,2,1,0:T(8,128)(2,1)S(1)}, bf16[16,3,256,128]{3,2,1,0:T(8,128)(2,1)}, u32[]{:S(2)}) copy-start(bf16[16,3,256,128]{3,2,1,0:T(8,128)(2,1)} %param.9) | copy-start | bytes 9437188
